TPU v7x, 256 devices: a whole 4x4x8 slice. The times are simulated.
256 devices in a mesh: tm: 32 (over x_lo, z, core), strip: 8 (over x_hi, y).
Axes of the slice: x: 4 (x_hi: 2, x_lo: 2; x = x_hi * 2 + x_lo), y: 4, z: 8, core: 2. Of those that a mesh axis runs over, the one named last changes fastest.
Arguments:
- movie: bfloat16 [4096, 65536], P('tm', 'strip'), may hold values from -6 to 6
- shifts: float32 [4096, 128], P('tm', 'strip'), may hold values from -1 to 1
- projection: bfloat16 [65536, 256], P('strip'), may hold values from -0.03125 to 0.03125
- footprints: bfloat16 [256, 65536], P(None, 'strip'), may hold values from -0.375 to 0.375
- quality: float32 [4096], replicated, may hold values from 0.1 to 1
- continuity: float32 [4096], replicated, may hold values from 0.5 to 1
- retention: float32 [256], replicated, may hold values from 0.9 to 1, as said below
Outputs:
- activity: float32 [256, 4096], P('strip', 'tm')
- residual: bfloat16 [4096, 65536], P('tm', 'strip')
Inputs may be any that keep to these rules, and one draw needn't show every extreme that they name: `retention`: each factor's kernel weight falls by this factor from one frame to the next, times continuity.
All inputs are finite; a program needn't handle non-finite values.
Results may differ from a plain program's by a relative error of at most 0.0053.
Values may be sent and summed in bfloat16 or wider, within the bound.
A program may use at most 128 MiB of HBM per device.

v0:
```python
import jax
import jax.numpy as jnp
from jax import lax
from jax.sharding import PartitionSpec as P

RADIUS = 1


def copy_for_each(shard, axis):
    peers = lax.axis_size(axis)
    return lax.all_to_all(
        jnp.broadcast_to(shard[None], (peers, *shard.shape)), axis, 0, 0, tiled=True
    )


def gathered_once(shard, axis):
    leaves = jax.tree.leaves(shard)
    sequence = sorted(range(len(leaves)), key=lambda k: -leaves[k].size)
    width = (1, *leaves[sequence[0]].shape)[-1]
    lines = [
        jnp.pad(leaves[k].reshape(-1), (0, -leaves[k].size % width)).reshape(-1, width)
        for k in sequence
    ]
    both, at, found = (copy_for_each(jnp.concatenate(lines), axis), 0, {})
    for k, line in zip(sequence, lines):
        section = both[:, at : at + len(line)].reshape(len(both), -1)
        found[k] = section[:, : leaves[k].size].reshape(-1, *leaves[k].shape)
        at += len(line)
    numbers = iter(range(len(leaves)))
    return jax.tree.map(lambda _: found[next(numbers)], shard)


def folded_in_pairs(pieces, combine):
    while len(jax.tree.leaves(pieces)[0]) > 1:
        pieces = jax.vmap(combine)(
            *(jax.tree.map(lambda part: part[side::2], pieces) for side in (0, 1))
        )
    return jax.tree.map(lambda part: part[0], pieces)


def entering_2(shard, axis, combine, identity, reverse):
    peers, index = (lax.axis_size(axis), lax.axis_index(axis))
    passed = jnp.arange(peers) > index if reverse else jnp.arange(peers) < index

    def kept(part, zero, own):
        part = jnp.where(
            passed.reshape(-1, *(1 for _ in own.shape)), part, jnp.asarray(zero, own.dtype)
        )
        return part[::-1] if reverse else part

    pieces = gathered_once(shard, axis)
    return folded_in_pairs(jax.tree.map(kept, pieces, identity, shard), combine)


def with_halo(block, sides, width):
    for axis, dim in sides:
        count = lax.axis_size(axis)
        forward = [(i, i + 1) for i in range(count - 1)]
        backward = [(target, source) for source, target in forward]
        low = lax.ppermute(
            lax.slice_in_dim(block, block.shape[dim] - width, None, axis=dim), axis, forward
        )
        high = lax.ppermute(lax.slice_in_dim(block, 0, width, axis=dim), axis, backward)
        block = jnp.concatenate([low, block, high], axis=dim)
    return block


def gathered_total(shard, axis):
    return lax.all_gather(shard, axis).sum(0)


def linear_join(earlier, later):
    return (
        earlier[0] * later[0],
        earlier[1] * later[0] + later[1],
        earlier[2] * later[0] + later[2],
    )


def smooth_carried(traces, decays, quality_part, continuity_part):
    transition = decays[:, None] * continuity_part[None, :]
    weighted = traces * quality_part[None, :]
    quality_rows = jnp.broadcast_to(quality_part[None, :], traces.shape)
    forward_pass = lax.associative_scan(linear_join, (transition, weighted, quality_rows), axis=1)
    behind = lax.associative_scan(
        linear_join,
        (transition, transition * weighted, transition * quality_rows),
        axis=1,
        reverse=True,
    )
    identity = (jnp.ones_like(decays), jnp.zeros_like(decays), jnp.zeros_like(decays))
    entering = entering_2(
        (forward_pass[0][:, -1], forward_pass[1][:, -1], forward_pass[2][:, -1]),
        "tm",
        linear_join,
        identity,
        False,
    )
    leaving = entering_2(
        (behind[0][:, 0], behind[1][:, 0], behind[2][:, 0]), "tm", linear_join, identity, True
    )
    ahead_sum = forward_pass[1] + forward_pass[0] * entering[1][:, None]
    ahead_norm = forward_pass[2] + forward_pass[0] * entering[2][:, None]
    behind_sum = behind[1] + behind[0] * leaving[1][:, None]
    behind_norm = behind[2] + behind[0] * leaving[2][:, None]
    later_sum = jnp.concatenate([behind_sum[:, 1:], leaving[1][:, None]], axis=1)
    later_norm = jnp.concatenate([behind_norm[:, 1:], leaving[2][:, None]], axis=1)
    return (ahead_sum + later_sum) / jnp.sqrt(ahead_norm + later_norm)


def body(movie, shifts, projection, footprints, quality, continuity, retention):
    frame_count, pixel_count = movie.shape
    row_count = shifts.shape[1]
    col_count = pixel_count // row_count
    frame_start = lax.axis_index("tm") * frame_count
    padded = with_halo(movie, (("strip", 1),), RADIUS * col_count)
    summed = jnp.zeros((frame_count, pixel_count), jnp.float32)
    for offset in range(-RADIUS, RADIUS + 1):
        weight = jnp.maximum(0.0, 1.0 - jnp.abs(shifts - offset))
        spread = jnp.repeat(weight, col_count, axis=1)
        begin = (RADIUS + offset) * col_count
        summed = summed + spread * padded[:, begin : begin + pixel_count]
    warped = summed.astype(jnp.bfloat16)
    partial_value = jnp.einsum("pk,tp->kt", projection, warped, preferred_element_type=jnp.float32)
    traces = gathered_total(partial_value, "strip")
    held_count = traces.shape[0]
    quality_part = lax.dynamic_slice_in_dim(quality, frame_start, frame_count)
    continuity_part = lax.dynamic_slice_in_dim(continuity, frame_start, frame_count)
    activity = smooth_carried(traces, retention, quality_part, continuity_part)
    activity_low = activity.astype(jnp.bfloat16)
    per_strip = held_count // lax.axis_size("strip")
    activity_share = lax.dynamic_slice_in_dim(
        activity, lax.axis_index("strip") * per_strip, per_strip, 0
    )
    rebuilt = jnp.einsum("kt,kp->tp", activity_low, footprints, preferred_element_type=jnp.float32)
    residual = (warped.astype(jnp.float32) - rebuilt).astype(jnp.bfloat16)
    return (activity_share, residual)


def solution(mesh):
    return jax.shard_map(
        body,
        mesh=mesh,
        in_specs=(
            P("tm", "strip"),
            P("tm", "strip"),
            P("strip", None),
            P(None, "strip"),
            P(),
            P(),
            P(),
        ),
        out_specs=(P("strip", "tm"), P("tm", "strip")),
        check_vma=False,
    )
```

profile of v0, /device:TPU:1, one launch (start us, length us, event | category | flops | bytes accessed | tf_op | source)
XLA Modules:
  0.0 199.2 jit_solution(1160708126669802621)
XLA Ops:
  7.2 1.0 fusion.41
  8.2 4.0 %collective-permute-start = (bf16[128,512]{1,0:T(8,128)(2,1)S(1)}, bf16[128,512]{1,0:T(8,128)(2,1)S(1)}, u32[]{:S(2)}, u32[]{:S(2)}) collective-permute-start(bf16[128,512]{1,0:T(8,128)(2,1)S(1)} %get-tuple-element.6), channel_id=1, source_target_pairs={{0,1},{1,2},{2,3},{3,4},{4,5},{5,6},{6,7},{8,9},{9,10},{10,11},{11... | collective-permute-start | bytes 393224 | tf_op jit(solution)/shard_map/ppermute | solution.py:60
  12.2 1.3 collective-permute-start.1
  13.5 0.7 subtract_maximum_fusion.2
  14.7 5.4 %copy.32 = f32[16,8,16,512]{3,1,2,0:T(8,128)} copy(f32[16,8,16,512]{3,2,1,0:T(8,128)S(1)} %bitcast.58) | data formatting | bytes 8388608
  20.6 5.4 %copy.33 = f32[16,8,16,512]{3,1,2,0:T(8,128)} copy(f32[16,8,16,512]{3,2,1,0:T(8,128)S(1)} %bitcast.59) | data formatting | bytes 8388608
  26.5 3.3 %copy.34 = f32[16,8,16,512]{3,1,2,0:T(8,128)S(1)} copy(f32[16,8,16,512]{3,2,1,0:T(8,128)S(1)} %bitcast.60) | data formatting | bytes 8388608
  30.2 1.5 add_convert_fusion
  32.4 1.5 convolution_bitcast_fusion
  33.9 0.8 dynamic_slice.9
  35.6 0.8 dynamic_slice.10
  37.4 51.0 %all-gather.3.cloned.1.call-done = f32[2048,128]{0,1:T(8,128)} async-done(((f32[256,128]{0,1:T(8,128)}), f32[2048,128]{0,1:T(8,128)}) %all-gather.3.cloned.1.call-update) | async-done | bytes 1048592 | tf_op jit(solution)/shard_map/all_gather | solution.py:69
  88.5 1.6 copy.35
  121.8 0.7 pad_maximum_fusion.35
  123.2 0.7 pad.290
  123.9 0.7 pad_maximum_fusion.33
  124.6 0.7 pad.262
  125.3 0.7 fusion.28
  126.0 0.7 pad_maximum_fusion.26
  126.7 0.7 pad_maximum_fusion.27
  128.1 0.7 fusion.24
  128.9 0.7 pad_maximum_fusion.20
  130.3 0.7 pad_maximum_fusion.19
  131.0 0.8 fusion.20
  134.1 0.7 pad_maximum_fusion.8
  135.5 0.7 pad_maximum_fusion.7
  136.3 0.7 fusion.6
  137.7 0.7 pad_maximum_fusion.2
  138.4 0.7 concatenate.146
  139.9 8.9 %all-to-all-start = ((f32[32,3,256]{2,1,0:T(4,128)}), f32[32,3,256]{2,1,0:T(4,128)}, u32[]{:S(2)}, u32[]{:S(2)}) async-start(f32[32,3,256]{2,1,0:T(4,128)} %broadcast_in_dim.69), calls=%async_computation | async-start | bytes 262144 | tf_op jit(solution)/shard_map/all_to_all | solution.py:11
  148.9 0.7 pad_maximum_fusion.38
  149.6 0.7 pad_maximum_fusion.36
  153.2 0.7 slice.1070
  155.9 0.9 add_multiply_fusion.1
  156.8 0.7 pad_maximum_fusion.4
  158.3 1.3 pad_maximum_fusion.6
  159.6 0.9 pad.341
  160.4 2.2 %pad.342 = f32[256,128]{0,1:T(8,128)} pad(f32[256,64]{0,1:T(8,128)} %add.645, f32[]{:T(128)} %constant.12.clone.1), padding=0_0_0x1_0_1 | pad | bytes 196612 | tf_op jit(solution)/shard_map/pad | solution.py:85
  162.6 0.7 add_bitcast_fusion
  164.6 0.9 add.647
  165.6 0.9 rev.6
  166.5 0.9 rev.7
  168.1 8.3 %all-to-all-start.1 = ((f32[32,3,256]{2,1,0:T(4,128)}), f32[32,3,256]{2,1,0:T(4,128)S(1)}, u32[]{:S(2)}, u32[]{:S(2)}) async-start(f32[32,3,256]{2,1,0:T(4,128)} %broadcast_in_dim.73), calls=%async_computation.1 | async-start | bytes 262144 | tf_op jit(solution)/shard_map/all_to_all | solution.py:11
  176.4 1.1 fusion.42
  177.6 0.7 fusion.16
  178.8 6.7 %all-to-all-done.1 = f32[32,3,256]{2,1,0:T(4,128)S(1)} async-done(((f32[32,3,256]{2,1,0:T(4,128)}), f32[32,3,256]{2,1,0:T(4,128)S(1)}, u32[]{:S(2)}, u32[]{:S(2)}) %all-to-all-start.1) | async-done | bytes 98336 | tf_op jit(solution)/shard_map/all_to_all | solution.py:11
  187.3 4.2 %fusion = bf16[128,8192]{1,0:T(8,128)(2,1)} fusion(bf16[256,8192]{1,0:T(8,128)(2,1)} %param.10, bf16[128,8192]{1,0:T(8,128)(2,1)S(1)} %add_convert_fusion, f32[256,128]{0,1:T(8,128)S(1)} %fusion.1), kind=kOutput, calls=%fused_computation.1 | convolution fusion | flops 540049408 | bytes 8519680 | tf_op jit(solution)/shard_map/kt,kp->tp/dot_general | solution.py:135
  191.6 0.7 copy.25
  (423 shorter events, 52.1 us)
Async XLA Ops:
  7.2 81.3 %all-gather.3.cloned.1.call-start = ((), (), s32[]{:S(2)}) async-start(), calls=%async_computation.2 | async-start | bytes 1179648 | tf_op jit(solution)/shard_map/all_gather | solution.py:69
  8.2 21.6 %collective-permute-start = (bf16[128,512]{1,0:T(8,128)(2,1)S(1)}, bf16[128,512]{1,0:T(8,128)(2,1)S(1)}, u32[]{:S(2)}, u32[]{:S(2)}) collective-permute-start(bf16[128,512]{1,0:T(8,128)(2,1)S(1)} %get-tuple-element.6), channel_id=1, source_target_pairs={{0,1},{1,2},{2,3},{3,4},{4,5},{5,6},{6,7},{8,9},{9,10},{10,11},{11... | collective-permute-start | bytes 393224 | tf_op jit(solution)/shard_map/ppermute | solution.py:60
  12.2 17.6 %collective-permute-start.1 = (bf16[128,512]{1,0:T(8,128)(2,1)S(1)}, bf16[128,512]{1,0:T(8,128)(2,1)S(1)}, u32[]{:S(2)}, u32[]{:S(2)}) collective-permute-start(bf16[128,512]{1,0:T(8,128)(2,1)S(1)} %get-tuple-element.7), channel_id=1, source_target_pairs={{1,0},{2,1},{3,2},{4,3},{5,4},{6,5},{7,6},{9,8},{10,9},{11,10},{12... | collective-permute-start | bytes 393224 | tf_op jit(solution)/shard_map/ppermute | solution.py:63
  26.1 3.7 %copy-start.3 = (bf16[128,8192]{1,0:T(8,128)(2,1)S(1)}, bf16[128,8192]{1,0:T(8,128)(2,1)}, u32[]{:S(2)}) copy-start(bf16[128,8192]{1,0:T(8,128)(2,1)} %param.7) | copy-start | bytes 6291460
  26.4 3.4 %copy-start = (f32[16,8,16,512]{3,1,2,0:T(8,128)S(1)}, f32[16,8,16,512]{3,1,2,0:T(8,128)}, u32[]{:S(2)}) copy-start(f32[16,8,16,512]{3,1,2,0:T(8,128)} %copy.32) | copy-start | bytes 12582916
  26.4 3.8 %copy-start.1 = (f32[16,8,16,512]{3,1,2,0:T(8,128)S(1)}, f32[16,8,16,512]{3,1,2,0:T(8,128)}, u32[]{:S(2)}) copy-start(f32[16,8,16,512]{3,1,2,0:T(8,128)} %copy.33) | copy-start | bytes 12582916
  30.2 2.2 %copy-start.2 = (bf16[8192,256]{1,0:T(8,128)(2,1)S(1)}, bf16[8192,256]{1,0:T(8,128)(2,1)}, u32[]{:S(2)}) copy-start(bf16[8192,256]{1,0:T(8,128)(2,1)} %param.9) | copy-start | bytes 12582916
  32.4 57.9 %copy-start.23 = (f32[256]{0:T(256)S(1)}, f32[256]{0:T(256)}, u32[]{:S(2)}) copy-start(f32[256]{0:T(256)} %param.13) | copy-start | bytes 3076
  34.7 55.8 %copy-start.22 = (f32[128]{0:T(128)}, f32[128]{0:T(128)S(1)}, u32[]{:S(2)}) copy-start(f32[128]{0:T(128)S(1)} %dynamic_slice.9) | copy-start | bytes 1540
  131.8 18.6 %copy-start.7 = (f32[256,3]{0,1:T(4,128)S(1)}, f32[256,3]{0,1:T(4,128)}, u32[]{:S(2)}) copy-start(f32[256,3]{0,1:T(4,128)} %slice.1057) | copy-start | bytes 9220
  131.8 18.6 %copy-start.8 = (f32[256,3]{0,1:T(4,128)S(1)}, f32[256,3]{0,1:T(4,128)}, u32[]{:S(2)}) copy-start(f32[256,3]{0,1:T(4,128)} %slice.1058) | copy-start | bytes 9220
  131.8 18.8 %copy-start.4 = (f32[256,7]{0,1:T(8,128)S(1)}, f32[256,7]{0,1:T(8,128)}, u32[]{:S(2)}) copy-start(f32[256,7]{0,1:T(8,128)} %slice.1060) | copy-start | bytes 21508
  131.8 18.8 %copy-start.5 = (f32[256,7]{0,1:T(8,128)S(1)}, f32[256,7]{0,1:T(8,128)}, u32[]{:S(2)}) copy-start(f32[256,7]{0,1:T(8,128)} %slice.1061) | copy-start | bytes 21508
  131.8 18.8 %copy-start.6 = (f32[256,7]{0,1:T(8,128)S(1)}, f32[256,7]{0,1:T(8,128)}, u32[]{:S(2)}) copy-start(f32[256,7]{0,1:T(8,128)} %slice.1115) | copy-start | bytes 21508
  133.2 15.6 %copy-start.10 = (f32[256,2]{0,1:T(2,128)S(1)}, f32[256,2]{0,1:T(2,128)}, u32[]{:S(2)}) copy-start(f32[256,2]{0,1:T(2,128)} %pad_add_fusion.2) | copy-start | bytes 6148
  133.2 16.3 %copy-start.12 = (f32[256,2]{0,1:T(2,128)S(1)}, f32[256,2]{0,1:T(2,128)}, u32[]{:S(2)}) copy-start(f32[256,2]{0,1:T(2,128)} %get-tuple-element.150) | copy-start | bytes 6148
  133.2 16.3 %copy-start.11 = (f32[256,2]{0,1:T(2,128)S(1)}, f32[256,2]{0,1:T(2,128)}, u32[]{:S(2)}) copy-start(f32[256,2]{0,1:T(2,128)} %get-tuple-element.149) | copy-start | bytes 6148
  133.3 17.1 %copy-start.9 = (f32[256,3]{0,1:T(4,128)S(1)}, f32[256,3]{0,1:T(4,128)}, u32[]{:S(2)}) copy-start(f32[256,3]{0,1:T(4,128)} %slice.1113) | copy-start | bytes 9220
  133.3 17.5 %copy-start.16 = (f32[256,1]{0,1:T(1,128)S(1)}, f32[256,1]{0,1:T(1,128)}, u32[]{:S(2)}) copy-start(f32[256,1]{0,1:T(1,128)} %slice.1275) | copy-start | bytes 3076
  133.3 17.6 %copy-start.15 = (f32[256,1]{0,1:T(1,128)S(1)}, f32[256,1]{0,1:T(1,128)}, u32[]{:S(2)}) copy-start(f32[256,1]{0,1:T(1,128)} %slice.1251) | copy-start | bytes 3076
  133.3 17.6 %copy-start.14 = (f32[256,1]{0,1:T(1,128)S(1)}, f32[256,1]{0,1:T(1,128)}, u32[]{:S(2)}) copy-start(f32[256,1]{0,1:T(1,128)} %slice.1297) | copy-start | bytes 3076
  133.3 17.7 %copy-start.13 = (f32[256,1]{0,1:T(1,128)S(1)}, f32[256,1]{0,1:T(1,128)}, u32[]{:S(2)}) copy-start(f32[256,1]{0,1:T(1,128)} %slice.1274) | copy-start | bytes 3076
  133.3 17.1 %copy-start.20 = (f32[256,1]{0,1:T(1,128)S(1)}, f32[256,1]{0,1:T(1,128)}, u32[]{:S(2)}) copy-start(f32[256,1]{0,1:T(1,128)} %slice.1299) | copy-start | bytes 3076
  133.3 17.2 %copy-start.19 = (f32[256,1]{0,1:T(1,128)S(1)}, f32[256,1]{0,1:T(1,128)}, u32[]{:S(2)}) copy-start(f32[256,1]{0,1:T(1,128)} %slice.1276) | copy-start | bytes 3076
  133.4 17.3 %copy-start.18 = (f32[256,1]{0,1:T(1,128)S(1)}, f32[256,1]{0,1:T(1,128)}, u32[]{:S(2)}) copy-start(f32[256,1]{0,1:T(1,128)} %slice.1252) | copy-start | bytes 3076
  133.4 17.4 %copy-start.17 = (f32[256,1]{0,1:T(1,128)S(1)}, f32[256,1]{0,1:T(1,128)}, u32[]{:S(2)}) copy-start(f32[256,1]{0,1:T(1,128)} %slice.1298) | copy-start | bytes 3076
  134.0 16.4 %copy-start.21 = (f32[256,1]{0,1:T(1,128)S(1)}, f32[256,1]{0,1:T(1,128)}, u32[]{:S(2)}) copy-start(f32[256,1]{0,1:T(1,128)} %slice.1253) | copy-start | bytes 3076
  139.9 27.6 %all-to-all-start = ((f32[32,3,256]{2,1,0:T(4,128)}), f32[32,3,256]{2,1,0:T(4,128)}, u32[]{:S(2)}, u32[]{:S(2)}) async-start(f32[32,3,256]{2,1,0:T(4,128)} %broadcast_in_dim.69), calls=%async_computation | async-start | bytes 262144 | tf_op jit(solution)/shard_map/all_to_all | solution.py:11
  168.1 17.3 %all-to-all-start.1 = ((f32[32,3,256]{2,1,0:T(4,128)}), f32[32,3,256]{2,1,0:T(4,128)S(1)}, u32[]{:S(2)}, u32[]{:S(2)}) async-start(f32[32,3,256]{2,1,0:T(4,128)} %broadcast_in_dim.73), calls=%async_computation.1 | async-start | bytes 262144 | tf_op jit(solution)/shard_map/all_to_all | solution.py:11
Sparse Core Ops, SparseCore 0:
  34.0 54.4 all-gather.2
where the time goes:
time: 201 us; the launch traced here: 199 us
  local copies, waits for them, and re-layouts  63.9 us (32%)
  waiting for transfers between devices  57.7 us (29%)
  other arithmetic  33.7 us (17%)
  starting transfers between devices  22.6 us (11%)
  between operations  15.6 us (8%)
  matrix products  5.69 us (3%)
    all_gather x1, waiting for transfers between devices, gathered_total(): return lax.all_gather(shard, axis).sum(0)  51 us
    unnamed x53, local copies, waits for them, and re-layouts  17.6 us
    all_to_all x2, starting transfers between devices, copy_for_each(): lax.all_to_all(jnp.broadcast_to(shard[None], (peers, *shard.shape)), axis...  17.2 us
    slice x65, local copies, waits for them, and re-layouts, smooth_carried(): lax.associative_scan(linear_join, (transition, weighted, quality_rows), a...  15.3 us
    slice x72, local copies, waits for them, and re-layouts, smooth_carried(): lax.associative_scan(linear_join, (transition, transition * weighted, tra...  14.9 us
    concatenate x16, other arithmetic, smooth_carried(): lax.associative_scan(linear_join, (transition, weighted, quality_rows), a...  10.8 us
    all_to_all x2, waiting for transfers between devices, copy_for_each(): lax.all_to_all(jnp.broadcast_to(shard[None], (peers, *shard.shape)), axis...  6.66 us
    concatenate x17, other arithmetic, smooth_carried(): lax.associative_scan(linear_join, (transition, transition * weighted, tra...  6.14 us
  transfers between devices with their start and end apart: 5, of which 2 were waited for; matrix products, arithmetic and copies ran while one was open for 20% of the time, Pallas kernels for 0%

commit v1 on v0

v1 whole, which is shorter than its diff:
```python
import functools

import jax
import jax.numpy as jnp
from jax import lax
from jax.experimental import pallas as pl
from jax.experimental.pallas import tpu as pltpu
from jax.sharding import PartitionSpec as P

MESH = pl.DeviceIdType.MESH
HI = lax.Precision.HIGHEST
F32 = jnp.float32
BF16 = jnp.bfloat16


def lane_shift(x, d, fill):
    n = x.shape[1]
    lane = lax.broadcasted_iota(jnp.int32, x.shape, 1)
    keep = lane >= d if d > 0 else lane < n + d
    return jnp.where(keep, pltpu.roll(x, d % n, 1), fill)


def row_shift(x, d, fill):
    n = x.shape[0]
    row = lax.broadcasted_iota(jnp.int32, x.shape, 0)
    keep = row >= d if d > 0 else row < n + d
    return jnp.where(keep, pltpu.roll(x, d % n, 0), fill)


def row_turn(x, d):
    n = x.shape[0]
    d = d % n
    if d % 8 == 0:
        return jnp.concatenate([x[n - d :], x[: n - d]], axis=0)
    return pltpu.roll(x, d, 0)


def kernel(
    tm_n, strip_n,
    movie_h, shifts_r, proj_h, foot_h, quality_r, cont_r, ret_r,
    act_h, res_h,
    movie_v, proj_v, foot_v, warp_v, halo_v, shift_v,
    col_v, rows_v, prefix_v, suffix_v, scale_v, coef_v, part_v,
    rs_v, all_v, tm_v, carry_v, out_v,
    load_sem, halo_send, halo_recv, rs_send, rs_recv, tm_send, tm_recv,
    ag_send, ag_recv, cs_send, cs_recv, out_sem,
):
    frames, pixels = movie_v.shape
    factors = proj_v.shape[1]
    rows = shifts_r.shape[0]
    cols = pixels // rows
    share = frames // strip_n
    steps = frames.bit_length() - 1
    me_t = lax.axis_index("tm")
    me_s = lax.axis_index("strip")
    halves = [slice(i, i + 128) for i in range(0, factors, 128)]

    chunks = 4
    wide = pixels // chunks
    loads = []
    for c in range(chunks):
        part = pl.ds(c * wide, wide)
        loads.append((
            pltpu.make_async_copy(movie_h.at[:, part], movie_v.at[:, part], load_sem.at[2 * c]),
            pltpu.make_async_copy(proj_h.at[part], proj_v.at[part], load_sem.at[2 * c + 1]),
        ))
    foot_load = pltpu.make_async_copy(foot_h, foot_v, load_sem.at[2 * chunks])
    for pair in loads:
        for copy in pair:
            copy.start()

    barrier = pltpu.get_barrier_semaphore()

    def hail_strip(d, _):
        pl.semaphore_signal(
            barrier, inc=1, device_id={"strip": lax.rem(me_s + d, strip_n)}, device_id_type=MESH
        )
        return 0

    def hail_tm(d, _):
        pl.semaphore_signal(
            barrier, inc=1, device_id={"tm": lax.rem(me_t + d, tm_n)}, device_id_type=MESH
        )
        return 0

    lax.fori_loop(1, strip_n, hail_strip, 0)
    lax.fori_loop(1, tm_n, hail_tm, 0)
    pl.semaphore_wait(barrier, strip_n - 1 + tm_n - 1)

    def halo_copy(side):
        source = pl.ds((rows - 1) * cols, cols) if side == 0 else pl.ds(0, cols)
        target = me_s + 1 if side == 0 else me_s - 1
        return pltpu.make_async_remote_copy(
            src_ref=movie_h.at[:, source], dst_ref=halo_v.at[side],
            send_sem=halo_send.at[side], recv_sem=halo_recv.at[side],
            device_id={"strip": target}, device_id_type=MESH,
        )

    @pl.when(me_s < strip_n - 1)
    def _():
        halo_copy(0).start()

    @pl.when(me_s > 0)
    def _():
        halo_copy(1).start()

    @pl.when(me_s == 0)
    def _():
        halo_v[0] = jnp.zeros((frames, cols), BF16)

    @pl.when(me_s == strip_n - 1)
    def _():
        halo_v[1] = jnp.zeros((frames, cols), BF16)

    shifts = jnp.concatenate([shifts_r[...], jnp.zeros((frames - rows, frames), F32)], axis=0).T
    for h in range(rows):
        shift_v[h] = jnp.broadcast_to(shifts[:, h : h + 1], (frames, 128))

    quality, cont = quality_r[...], cont_r[...]
    ret = ret_r[...]
    powers = [ret]
    for _ in range(steps):
        powers.append(powers[-1] * powers[-1])
    prefix, suffix = cont, cont
    for level in range(steps):
        d = 1 << level
        prefix = prefix * lane_shift(prefix, d, 1.0)
        suffix = suffix * lane_shift(suffix, -d, 1.0)
    after = lane_shift(suffix, -1, 1.0)
    rows_v[0] = quality
    rows_v[1] = cont
    rows_v[2] = prefix
    rows_v[3] = after
    mine = [rows_v[i, pl.ds(me_t, 1), :] for i in range(4)]
    lane = lax.broadcasted_iota(jnp.int32, (1, frames), 1)
    ahead, behind = mine[1], mine[1]
    ahead_rows, behind_rows = [], []
    for level in range(steps):
        d = 1 << level
        ahead_rows.append(jnp.where(lane >= d, ahead, 0.0))
        behind_rows.append(jnp.where(lane < frames - d, behind, 0.0))
        ahead = ahead * lane_shift(ahead, d, 1.0)
        behind = behind * lane_shift(behind, -d, 1.0)
    lines = ahead_rows + behind_rows + mine
    lines = jnp.concatenate(lines + [jnp.zeros((frames - len(lines), frames), F32)], axis=0)
    turned = lines.T
    for i in range(2 * steps + 4):
        col_v[i] = jnp.broadcast_to(turned[:, i : i + 1], (frames, 128))
    QUALITY, CONT, PREFIX, AFTER = (2 * steps + i for i in range(4))

    small = [jnp.ones_like(ret), ret, powers[1], powers[1] * ret, powers[2]]
    small += [powers[2] * small[i] for i in (1, 2, 3)]
    rising = jnp.concatenate(small[1:] + [powers[3]], axis=0)
    falling = jnp.concatenate(small[::-1], axis=0)
    for level in range(3, steps):
        rising = jnp.concatenate([rising, rising * powers[level]], axis=0)
        falling = jnp.concatenate([falling * powers[level], falling], axis=0)
    for h in halves:
        prefix_v[:, h] = col_v[PREFIX] * rising[:, h]
        suffix_v[:, h] = col_v[AFTER] * falling[:, h]

    whole = prefix[:, frames - 1 : frames] * powers[steps]
    block = lax.broadcasted_iota(jnp.int32, (tm_n, factors), 0)
    before = jnp.where(block < me_t, whole, 1.0)
    beyond = jnp.where(block > me_t, whole, 1.0)
    d = 1
    while d < tm_n:
        before = before * row_shift(before, -d, 1.0)
        beyond = beyond * row_shift(beyond, d, 1.0)
        d *= 2
    before = jnp.where(block < me_t, row_shift(before, -1, 1.0), 0.0)
    beyond = jnp.where(block > me_t, row_shift(beyond, 1, 1.0), 0.0)
    for i, h in enumerate(halves):
        coef_v[i] = before[:, h]
        coef_v[len(halves) + i] = beyond[:, h]
    norm_in = jnp.sum(
        before * jnp.dot(quality * after, falling, precision=HI, preferred_element_type=F32),
        axis=0, keepdims=True,
    )
    norm_out = jnp.sum(
        beyond * jnp.dot(quality * prefix, rising, precision=HI, preferred_element_type=F32),
        axis=0, keepdims=True,
    )

    def smoothed(x, h):
        fore = x
        back = x * (col_v[CONT] * ret[:, h])
        for level in range(steps):
            d = 1 << level
            fore = fore + (col_v[level] * powers[level][:, h]) * row_turn(fore, d)
            back = back + (col_v[steps + level] * powers[level][:, h]) * row_turn(back, -d)
        row = lax.broadcasted_iota(jnp.int32, back.shape, 0)
        return fore + jnp.where(row < frames - 1, row_turn(back, -1), 0.0)

    for h in halves:
        norm = smoothed(col_v[QUALITY], h)
        norm = norm + prefix_v[:, h] * norm_in[:, h] + suffix_v[:, h] * norm_out[:, h]
        scale_v[:, h] = 1.0 / jnp.sqrt(norm)

    def warp_row(h, above, own, below):
        s = shift_v[h]
        near = jnp.abs(s)
        keep = jnp.maximum(0.0, 1.0 - near)
        down = s > 0.0
        for w in range(0, cols, 128):
            w = slice(w, w + 128)
            other = jnp.where(down, below[:, w].astype(F32), above[:, w].astype(F32))
            warped = keep * own[:, w].astype(F32) + near * other
            yield w, warped.astype(BF16)

    def row_ref(h):
        return movie_v.at[:, pl.ds(pl.multiple_of(h * cols, cols), cols)]

    def do_row(h, above, below):
        at = pl.multiple_of(h * cols, cols)
        for w, warped in warp_row(h, above[...], row_ref(h)[...], below[...]):
            warp_v[:, pl.ds(at + w.start, 128)] = warped
        part_v[...] += jnp.dot(
            warp_v[:, pl.ds(at, cols)], proj_v[pl.ds(at, cols), :], preferred_element_type=F32
        )

    part_v[...] = jnp.zeros((frames, factors), F32)
    done = 1
    for c in range(chunks):
        for copy in loads[c]:
            copy.wait()
        last = (c + 1) * rows // chunks - 1

        def inner(h, _):
            do_row(h, row_ref(h - 1), row_ref(h + 1))
            return 0

        lax.fori_loop(done, last, inner, 0)
        done = last
    foot_load.start()

    @pl.when(me_s > 0)
    def _():
        halo_copy(0).wait_recv()

    do_row(0, halo_v.at[0], row_ref(1))

    @pl.when(me_s < strip_n - 1)
    def _():
        halo_copy(1).wait_recv()

    do_row(rows - 1, row_ref(rows - 2), halo_v.at[1])

    def strip_peer(d):
        return lax.rem(me_s + d, strip_n)

    def rs_copy(peer):
        return pltpu.make_async_remote_copy(
            src_ref=part_v.at[pl.ds(pl.multiple_of(peer * share, share), share)],
            dst_ref=rs_v.at[me_s], send_sem=rs_send.at[peer], recv_sem=rs_recv.at[me_s],
            device_id={"strip": peer}, device_id_type=MESH,
        )

    def tm_copy(peer):
        return pltpu.make_async_remote_copy(
            src_ref=tm_v.at[me_t], dst_ref=tm_v.at[me_t],
            send_sem=tm_send.at[peer], recv_sem=tm_recv.at[me_t],
            device_id={"tm": peer}, device_id_type=MESH,
        )

    def ag_copy(peer):
        mine = pl.ds(pl.multiple_of(me_s * share, share), share)
        return pltpu.make_async_remote_copy(
            src_ref=all_v.at[mine], dst_ref=all_v.at[mine],
            send_sem=ag_send.at[peer], recv_sem=ag_recv.at[me_s],
            device_id={"strip": peer}, device_id_type=MESH,
        )

    def cs_copy(peer):
        return pltpu.make_async_remote_copy(
            src_ref=carry_v.at[me_s], dst_ref=carry_v.at[me_s],
            send_sem=cs_send.at[peer], recv_sem=cs_recv.at[me_s],
            device_id={"strip": peer}, device_id_type=MESH,
        )

    def each(count, start, make, act):
        def one(d, _):
            act(make(lax.rem(start + d, count)))
            return 0

        lax.fori_loop(1, count, one, 0)

    for i, h in enumerate(halves):
        weighted = part_v[:, h] * col_v[QUALITY]
        tm_v[me_t, i : i + 1] = jnp.sum(weighted * suffix_v[:, h], axis=0, keepdims=True)
        j = len(halves) + i
        tm_v[me_t, j : j + 1] = jnp.sum(weighted * prefix_v[:, h], axis=0, keepdims=True)
    each(strip_n, me_s, rs_copy, lambda copy: copy.start())
    each(tm_n, me_t, tm_copy, lambda copy: copy.start())

    def arrived(slot, ref, sem, **axis):
        pltpu.make_async_remote_copy(
            src_ref=ref, dst_ref=ref, send_sem=sem, recv_sem=sem,
            device_id=axis, device_id_type=MESH,
        ).wait_recv()

    rs_v[me_s] = part_v[pl.ds(pl.multiple_of(me_s * share, share), share), :]
    each(
        strip_n, me_s, lambda peer: peer,
        lambda peer: arrived(peer, rs_v.at[peer], rs_recv.at[peer], strip=peer),
    )
    total = rs_v[0]
    for i in range(1, strip_n):
        total = total + rs_v[i]
    all_v[pl.ds(pl.multiple_of(me_s * share, share), share), :] = total
    each(strip_n, me_s, ag_copy, lambda copy: copy.start())

    each(
        tm_n, me_t, lambda peer: peer,
        lambda peer: arrived(peer, tm_v.at[peer], tm_recv.at[peer], tm=peer),
    )
    for i in range(2 * len(halves)):
        carry_v[me_s, i : i + 1] = jnp.sum(coef_v[i] * tm_v[:, i, :], axis=0, keepdims=True)
    each(strip_n, me_s, cs_copy, lambda copy: copy.start())

    def share_of(peer):
        return all_v.at[pl.ds(pl.multiple_of(peer * share, share), share)]

    each(
        strip_n, me_s, lambda peer: peer,
        lambda peer: arrived(peer, share_of(peer), ag_recv.at[peer], strip=peer),
    )
    sums = []
    for h in halves:
        sums.append(smoothed(all_v[:, h] * col_v[QUALITY], h))
    each(
        strip_n, me_s, lambda peer: peer,
        lambda peer: arrived(peer, carry_v.at[peer], cs_recv.at[peer], strip=peer),
    )
    carried = carry_v[0]
    for i in range(1, strip_n):
        carried = carried + carry_v[i]
    low = []
    for i, h in enumerate(halves):
        j = len(halves) + i
        value = sums[i] + prefix_v[:, h] * carried[i : i + 1] + suffix_v[:, h] * carried[j : j + 1]
        value = value * scale_v[:, h]
        out_v[h, :] = value.T
        low.append(value.astype(BF16))
    low = jnp.concatenate(low, axis=1)
    per = factors // strip_n
    act_copy = pltpu.make_async_copy(
        out_v.at[pl.ds(pl.multiple_of(me_s * per, per), per)], act_h, out_sem.at[chunks]
    )
    act_copy.start()

    foot_load.wait()
    writes = []
    for c in range(chunks):

        def subtract(n, _):
            at = pl.ds(pl.multiple_of(n * cols, cols), cols)
            rebuilt = jnp.dot(low, foot_v[:, at], preferred_element_type=F32)
            warp_v[:, at] = (warp_v[:, at].astype(F32) - rebuilt).astype(BF16)
            return 0

        lax.fori_loop(c * rows // chunks, (c + 1) * rows // chunks, subtract, 0)
        part = pl.ds(c * wide, wide)
        copy = pltpu.make_async_copy(warp_v.at[:, part], res_h.at[:, part], out_sem.at[c])
        copy.start()
        writes.append(copy)

    @pl.when(me_s < strip_n - 1)
    def _():
        halo_copy(0).wait_send()

    @pl.when(me_s > 0)
    def _():
        halo_copy(1).wait_send()

    each(strip_n, me_s, rs_copy, lambda copy: copy.wait_send())
    each(tm_n, me_t, tm_copy, lambda copy: copy.wait_send())
    each(strip_n, me_s, ag_copy, lambda copy: copy.wait_send())
    each(strip_n, me_s, cs_copy, lambda copy: copy.wait_send())
    act_copy.wait()
    for copy in writes:
        copy.wait()


def body(tm_n, strip_n, movie, shifts, projection, footprints, quality, continuity, retention):
    frames, pixels = movie.shape
    factors = projection.shape[1]
    rows = shifts.shape[1]
    cols = pixels // rows
    per = factors // strip_n
    share = frames // strip_n
    halves = factors // 128
    steps = frames.bit_length() - 1
    DMA = pltpu.SemaphoreType.DMA
    vmem = pl.BlockSpec(memory_space=pltpu.VMEM)
    hbm = pl.BlockSpec(memory_space=pl.ANY)
    return pl.pallas_call(
        functools.partial(kernel, tm_n, strip_n),
        out_shape=(
            jax.ShapeDtypeStruct((per, frames), F32),
            jax.ShapeDtypeStruct((frames, pixels), BF16),
        ),
        in_specs=[hbm, vmem, hbm, hbm, vmem, vmem, vmem],
        out_specs=(hbm, hbm),
        scratch_shapes=[
            pltpu.VMEM((frames, pixels), BF16),
            pltpu.VMEM((pixels, factors), BF16),
            pltpu.VMEM((factors, pixels), BF16),
            pltpu.VMEM((frames, pixels), BF16),
            pltpu.VMEM((2, frames, cols), BF16),
            pltpu.VMEM((rows, frames, 128), F32),
            pltpu.VMEM((2 * steps + 4, frames, 128), F32),
            pltpu.VMEM((4, tm_n, frames), F32),
            pltpu.VMEM((frames, factors), F32),
            pltpu.VMEM((frames, factors), F32),
            pltpu.VMEM((frames, factors), F32),
            pltpu.VMEM((2 * halves, tm_n, 128), F32),
            pltpu.VMEM((frames, factors), F32),
            pltpu.VMEM((strip_n, share, factors), F32),
            pltpu.VMEM((frames, factors), F32),
            pltpu.VMEM((tm_n, 2 * halves, 128), F32),
            pltpu.VMEM((strip_n, 2 * halves, 128), F32),
            pltpu.VMEM((factors, frames), F32),
            DMA((9,)), DMA((2,)), DMA((2,)),
            DMA((strip_n,)), DMA((strip_n,)), DMA((tm_n,)), DMA((tm_n,)),
            DMA((strip_n,)), DMA((strip_n,)), DMA((strip_n,)), DMA((strip_n,)),
            DMA((5,)),
        ],
        compiler_params=pltpu.CompilerParams(collective_id=0, has_side_effects=True),
    )(
        movie, shifts.T, projection, footprints,
        quality.reshape(tm_n, frames), continuity.reshape(tm_n, frames), retention.reshape(1, factors),
    )


def solution(mesh):
    return jax.shard_map(
        functools.partial(body, mesh.shape["tm"], mesh.shape["strip"]),
        mesh=mesh,
        in_specs=(
            P("tm", "strip"), P("tm", "strip"), P("strip", None), P(None, "strip"), P(), P(), P(),
        ),
        out_specs=(P("strip", "tm"), P("tm", "strip")),
        check_vma=False,
    )
```

time: 201 us -> 38.5 us (0.19)
  local copies, waits for them, and re-layouts: 63.9 us -> 4.42 us
  waiting for transfers between devices: 57.7 us -> 0 us
  other arithmetic: 33.7 us -> 0 us
  Pallas kernels: 0 us -> 33.2 us
  starting transfers between devices: 22.6 us -> 0 us
  between operations: 15.6 us -> 0.64 us
  matrix products: 5.69 us -> 0 us
    all_gather x1 -> x0, waiting for transfers between devices: 51 us -> none  [gathered_total(): return lax.all_gather(shard, axis).sum(0)]
    slice x194 -> x0, local copies, waits for them, and re-layouts: 33.7 us -> none  [the longest x65 15.3 us: smooth_carried(): lax.associative_scan(linear_join, (transition, weighted, quality_rows), a...]
    pallas_call x0 -> x1, Pallas kernels: none -> 33.2 us  [body(): pl.pallas_call(functools.partial(kernel, tm_n, strip_n), out_shape=(jax.S...]
    all_to_all x2 -> x0, starting transfers between devices: 17.2 us -> none  [copy_for_each(): lax.all_to_all(jnp.broadcast_to(shard[None], (peers, *shard.shape)), axis...]
    concatenate x35 -> x0, other arithmetic: 17 us -> none  [the longest x16 10.8 us: smooth_carried(): lax.associative_scan(linear_join, (transition, weighted, quality_rows), a...]
    unnamed x53 -> x2, local copies, waits for them, and re-layouts: 17.6 us -> 4.42 us
    add x66 -> x0, other arithmetic: 8.71 us -> none  [the longest x20 4.16 us: smooth_carried(): lax.associative_scan(linear_join, (transition, transition * weighted, tra...]
    all_to_all x2 -> x0, waiting for transfers between devices: 6.66 us -> none  [copy_for_each(): lax.all_to_all(jnp.broadcast_to(shard[None], (peers, *shard.shape)), axis...]
  transfers between devices with their start and end apart: 5 -> 0, of which waited for: 2 -> 0; matrix products, arithmetic and copies ran while one was open for 20% -> 0% of each run, Pallas kernels for 0% -> 0%
where the time goes in v1:
time: 38.5 us; the launch traced here: 38.2 us
  Pallas kernels  33.2 us (86%)
  local copies, waits for them, and re-layouts  4.42 us (11%)
  between operations  0.64 us (2%)
    pallas_call x1, Pallas kernels, body(): pl.pallas_call(functools.partial(kernel, tm_n, strip_n), out_shape=(jax.S...  33.2 us
    unnamed x2, local copies, waits for them, and re-layouts  4.42 us

profile of v1, /device:TPU:1, one launch (start us, length us, event | category | flops | bytes accessed | tf_op | source)
XLA Modules:
  0.0 38.2 jit_solution(16296997241828147673)
XLA Ops:
  0.6 33.2 %shard_map.86 = (f32[32,128]{1,0:T(8,128)}, bf16[128,8192]{1,0:T(8,128)(2,1)}) custom-call(bf16[128,8192]{1,0:T(8,128)(2,1)} %movie_h.1, f32[16,128]{1,0:T(8,128)} %bitcast.6, bf16[8192,256]{1,0:T(8,128)(2,1)} %proj_h.1, bf16[256,8192]{1,0:T(8,128)(2,1)} %foot_h.1, f32[32,128]{1,0:T(8,128)} %bitcast.4, f32[32,128]{1,0:T(8,128)} %bitcast.5, f32[1,256]{1,0:T(1,128)} %bitcast.7), custom_call_target="tpu_custom_call" | custom-call | tf_op jit(solution)/shard_map/pallas_call | solution.py:397
  33.8 1.3 %copy.11 = f32[32,128]{1,0:T(8,128)} copy(f32[32,128]{1,0:T(8,128)} %get-tuple-element.4) | data formatting | bytes 32768
  35.1 3.1 %copy.12 = bf16[128,8192]{1,0:T(8,128)(2,1)} copy(bf16[128,8192]{1,0:T(8,128)(2,1)} %get-tuple-element.5) | data formatting | bytes 4194304

commit v2 on v1

v2 whole, which is shorter than its diff:
```python
import functools

import jax
import jax.numpy as jnp
from jax import lax
from jax.experimental import pallas as pl
from jax.experimental.pallas import tpu as pltpu
from jax.sharding import PartitionSpec as P

MESH = pl.DeviceIdType.MESH
HI = lax.Precision.HIGHEST
F32 = jnp.float32
BF16 = jnp.bfloat16


def lane_shift(x, d, fill):
    n = x.shape[1]
    lane = lax.broadcasted_iota(jnp.int32, x.shape, 1)
    keep = lane >= d if d > 0 else lane < n + d
    return jnp.where(keep, pltpu.roll(x, d % n, 1), fill)


def row_shift(x, d, fill):
    n = x.shape[0]
    row = lax.broadcasted_iota(jnp.int32, x.shape, 0)
    keep = row >= d if d > 0 else row < n + d
    return jnp.where(keep, pltpu.roll(x, d % n, 0), fill)


def row_turn(x, d):
    n = x.shape[0]
    d = d % n
    if d % 8 == 0:
        return jnp.concatenate([x[n - d :], x[: n - d]], axis=0)
    return pltpu.roll(x, d, 0)


def kernel(
    tm_n, strip_n,
    movie_h, shifts_h, proj_h, foot_h, quality_h, cont_h, ret_h,
    low_v, warp_v, foot_v, act_v,
    movie_v, proj_v, halo_v, shift_v, shifts_r, quality_r, cont_r, ret_r,
    col_v, rows_v, prefix_v, suffix_v, scale_v, coef_v, part_v,
    rs_v, all_v, tm_v, carry_v, out_v,
    load_sem, halo_send, halo_recv, rs_send, rs_recv, tm_send, tm_recv,
    ag_send, ag_recv, cs_send, cs_recv,
):
    frames, pixels = movie_v.shape
    factors = proj_v.shape[1]
    rows = shifts_r.shape[0]
    cols = pixels // rows
    share = frames // strip_n
    steps = frames.bit_length() - 1
    me_t = lax.axis_index("tm")
    me_s = lax.axis_index("strip")
    halves = [slice(i, i + 128) for i in range(0, factors, 128)]

    barrier = pltpu.get_barrier_semaphore()

    def hail_strip(d, _):
        pl.semaphore_signal(
            barrier, inc=1, device_id={"strip": lax.rem(me_s + d, strip_n)}, device_id_type=MESH
        )
        return 0

    def hail_tm(d, _):
        pl.semaphore_signal(
            barrier, inc=1, device_id={"tm": lax.rem(me_t + d, tm_n)}, device_id_type=MESH
        )
        return 0

    lax.fori_loop(1, strip_n, hail_strip, 0)
    lax.fori_loop(1, tm_n, hail_tm, 0)

    small = [
        pltpu.make_async_copy(source, target, load_sem.at[i])
        for i, (source, target) in enumerate(
            ((shifts_h, shifts_r), (quality_h, quality_r), (cont_h, cont_r), (ret_h, ret_r))
        )
    ]
    large = [
        pltpu.make_async_copy(movie_h, movie_v, load_sem.at[4]),
        pltpu.make_async_copy(proj_h, proj_v, load_sem.at[5]),
    ]
    foot_load = pltpu.make_async_copy(foot_h, foot_v, load_sem.at[6])
    for copy in small + large:
        copy.start()
    pl.semaphore_wait(barrier, strip_n - 1 + tm_n - 1)

    def halo_copy(side):
        source = pl.ds((rows - 1) * cols, cols) if side == 0 else pl.ds(0, cols)
        target = me_s + 1 if side == 0 else me_s - 1
        return pltpu.make_async_remote_copy(
            src_ref=movie_h.at[:, source], dst_ref=halo_v.at[side],
            send_sem=halo_send.at[side], recv_sem=halo_recv.at[side],
            device_id={"strip": target}, device_id_type=MESH,
        )

    @pl.when(me_s < strip_n - 1)
    def _():
        halo_copy(0).start()

    @pl.when(me_s > 0)
    def _():
        halo_copy(1).start()

    @pl.when(me_s == 0)
    def _():
        halo_v[0] = jnp.zeros((frames, cols), BF16)

    @pl.when(me_s == strip_n - 1)
    def _():
        halo_v[1] = jnp.zeros((frames, cols), BF16)

    for copy in small:
        copy.wait()

    shifts = jnp.concatenate([shifts_r[...], jnp.zeros((frames - rows, frames), F32)], axis=0).T
    for h in range(rows):
        shift_v[h] = jnp.broadcast_to(shifts[:, h : h + 1], (frames, 128))

    quality, cont = quality_r[...], cont_r[...]
    ret = ret_r[...]
    powers = [ret]
    for _ in range(steps):
        powers.append(powers[-1] * powers[-1])
    prefix, suffix = cont, cont
    for level in range(steps):
        d = 1 << level
        prefix = prefix * lane_shift(prefix, d, 1.0)
        suffix = suffix * lane_shift(suffix, -d, 1.0)
    after = lane_shift(suffix, -1, 1.0)
    rows_v[0] = quality
    rows_v[1] = cont
    rows_v[2] = prefix
    rows_v[3] = after
    mine = [rows_v[i, pl.ds(me_t, 1), :] for i in range(4)]
    lane = lax.broadcasted_iota(jnp.int32, (1, frames), 1)
    ahead, behind = mine[1], mine[1]
    ahead_rows, behind_rows = [], []
    for level in range(steps):
        d = 1 << level
        ahead_rows.append(jnp.where(lane >= d, ahead, 0.0))
        behind_rows.append(jnp.where(lane < frames - d, behind, 0.0))
        ahead = ahead * lane_shift(ahead, d, 1.0)
        behind = behind * lane_shift(behind, -d, 1.0)
    lines = ahead_rows + behind_rows + mine
    lines = jnp.concatenate(lines + [jnp.zeros((frames - len(lines), frames), F32)], axis=0)
    turned = lines.T
    for i in range(2 * steps + 4):
        col_v[i] = jnp.broadcast_to(turned[:, i : i + 1], (frames, 128))
    QUALITY, CONT, PREFIX, AFTER = (2 * steps + i for i in range(4))

    small = [jnp.ones_like(ret), ret, powers[1], powers[1] * ret, powers[2]]
    small += [powers[2] * small[i] for i in (1, 2, 3)]
    rising = jnp.concatenate(small[1:] + [powers[3]], axis=0)
    falling = jnp.concatenate(small[::-1], axis=0)
    for level in range(3, steps):
        rising = jnp.concatenate([rising, rising * powers[level]], axis=0)
        falling = jnp.concatenate([falling * powers[level], falling], axis=0)
    for h in halves:
        prefix_v[:, h] = col_v[PREFIX] * rising[:, h]
        suffix_v[:, h] = col_v[AFTER] * falling[:, h]

    def warp_row(h, above, own, below):
        s = shift_v[h]
        near = jnp.abs(s)
        keep = jnp.maximum(0.0, 1.0 - near)
        down = s > 0.0
        for w in range(0, cols, 128):
            w = slice(w, w + 128)
            other = jnp.where(down, below[:, w].astype(F32), above[:, w].astype(F32))
            warped = keep * own[:, w].astype(F32) + near * other
            yield w, warped.astype(BF16)

    def row_ref(h):
        return movie_v.at[:, h * cols : (h + 1) * cols]

    def warp_into(h, above, below):
        for w, warped in warp_row(h, above[...], row_ref(h)[...], below[...]):
            warp_v[:, h * cols + w.start : h * cols + w.stop] = warped

    def project(first, last):
        at = slice(first * cols, last * cols)
        return jnp.dot(warp_v[:, at], proj_v[at, :], preferred_element_type=F32)

    for copy in large:
        copy.wait()
    group = 4
    for first in range(1, rows - 1, group):
        last = min(first + group, rows - 1)
        for h in range(first, last):
            warp_into(h, row_ref(h - 1), row_ref(h + 1))
        inner = project(first, last)
        part_v[...] = inner if first == 1 else part_v[...] + inner
    foot_load.start()

    @pl.when(me_s > 0)
    def _():
        halo_copy(0).wait_recv()

    warp_into(0, halo_v.at[0], row_ref(1))
    part_v[...] += project(0, 1)

    @pl.when(me_s < strip_n - 1)
    def _():
        halo_copy(1).wait_recv()

    warp_into(rows - 1, row_ref(rows - 2), halo_v.at[1])
    part_v[...] += project(rows - 1, rows)

    def strip_peer(d):
        return lax.rem(me_s + d, strip_n)

    def rs_copy(peer):
        return pltpu.make_async_remote_copy(
            src_ref=part_v.at[pl.ds(pl.multiple_of(peer * share, share), share)],
            dst_ref=rs_v.at[me_s], send_sem=rs_send.at[peer], recv_sem=rs_recv.at[me_s],
            device_id={"strip": peer}, device_id_type=MESH,
        )

    def tm_copy(peer):
        return pltpu.make_async_remote_copy(
            src_ref=tm_v.at[me_t], dst_ref=tm_v.at[me_t],
            send_sem=tm_send.at[peer], recv_sem=tm_recv.at[me_t],
            device_id={"tm": peer}, device_id_type=MESH,
        )

    def ag_copy(peer):
        mine = pl.ds(pl.multiple_of(me_s * share, share), share)
        return pltpu.make_async_remote_copy(
            src_ref=all_v.at[mine], dst_ref=all_v.at[mine],
            send_sem=ag_send.at[peer], recv_sem=ag_recv.at[me_s],
            device_id={"strip": peer}, device_id_type=MESH,
        )

    def cs_copy(peer):
        return pltpu.make_async_remote_copy(
            src_ref=carry_v.at[me_s], dst_ref=carry_v.at[me_s],
            send_sem=cs_send.at[peer], recv_sem=cs_recv.at[me_s],
            device_id={"strip": peer}, device_id_type=MESH,
        )

    def each(count, start, make, act):
        def one(d, _):
            act(make(lax.rem(start + d, count)))
            return 0

        lax.fori_loop(1, count, one, 0)

    for i, h in enumerate(halves):
        weighted = part_v[:, h] * col_v[QUALITY]
        tm_v[me_t, i : i + 1] = jnp.sum(weighted * suffix_v[:, h], axis=0, keepdims=True)
        j = len(halves) + i
        tm_v[me_t, j : j + 1] = jnp.sum(weighted * prefix_v[:, h], axis=0, keepdims=True)
    each(strip_n, me_s, rs_copy, lambda copy: copy.start())
    each(tm_n, me_t, tm_copy, lambda copy: copy.start())

    def arrived(slot, ref, sem, **axis):
        pltpu.make_async_remote_copy(
            src_ref=ref, dst_ref=ref, send_sem=sem, recv_sem=sem,
            device_id=axis, device_id_type=MESH,
        ).wait_recv()

    whole = prefix[:, frames - 1 : frames] * powers[steps]
    block = lax.broadcasted_iota(jnp.int32, (tm_n, factors), 0)
    before = jnp.where(block < me_t, whole, 1.0)
    beyond = jnp.where(block > me_t, whole, 1.0)
    d = 1
    while d < tm_n:
        before = before * row_shift(before, -d, 1.0)
        beyond = beyond * row_shift(beyond, d, 1.0)
        d *= 2
    before = jnp.where(block < me_t, row_shift(before, -1, 1.0), 0.0)
    beyond = jnp.where(block > me_t, row_shift(beyond, 1, 1.0), 0.0)
    for i, h in enumerate(halves):
        coef_v[i] = before[:, h]
        coef_v[len(halves) + i] = beyond[:, h]
    norm_in = jnp.sum(
        before * jnp.dot(quality * after, falling, precision=HI, preferred_element_type=F32),
        axis=0, keepdims=True,
    )
    norm_out = jnp.sum(
        beyond * jnp.dot(quality * prefix, rising, precision=HI, preferred_element_type=F32),
        axis=0, keepdims=True,
    )

    rs_v[me_s] = part_v[pl.ds(pl.multiple_of(me_s * share, share), share), :]
    each(
        strip_n, me_s, lambda peer: peer,
        lambda peer: arrived(peer, rs_v.at[peer], rs_recv.at[peer], strip=peer),
    )
    total = rs_v[0]
    for i in range(1, strip_n):
        total = total + rs_v[i]
    all_v[pl.ds(pl.multiple_of(me_s * share, share), share), :] = total
    each(strip_n, me_s, ag_copy, lambda copy: copy.start())

    def smoothed(x, h):
        fore = x
        back = x * (col_v[CONT] * ret[:, h])
        for level in range(steps):
            d = 1 << level
            fore = fore + (col_v[level] * powers[level][:, h]) * row_turn(fore, d)
            back = back + (col_v[steps + level] * powers[level][:, h]) * row_turn(back, -d)
        row = lax.broadcasted_iota(jnp.int32, back.shape, 0)
        return fore + jnp.where(row < frames - 1, row_turn(back, -1), 0.0)

    for h in halves:
        norm = smoothed(col_v[QUALITY], h)
        norm = norm + prefix_v[:, h] * norm_in[:, h] + suffix_v[:, h] * norm_out[:, h]
        scale_v[:, h] = 1.0 / jnp.sqrt(norm)

    each(
        tm_n, me_t, lambda peer: peer,
        lambda peer: arrived(peer, tm_v.at[peer], tm_recv.at[peer], tm=peer),
    )
    for i in range(2 * len(halves)):
        carry_v[me_s, i : i + 1] = jnp.sum(coef_v[i] * tm_v[:, i, :], axis=0, keepdims=True)
    each(strip_n, me_s, cs_copy, lambda copy: copy.start())

    def share_of(peer):
        return all_v.at[pl.ds(pl.multiple_of(peer * share, share), share)]

    each(
        strip_n, me_s, lambda peer: peer,
        lambda peer: arrived(peer, share_of(peer), ag_recv.at[peer], strip=peer),
    )
    sums = []
    for h in halves:
        sums.append(smoothed(all_v[:, h] * col_v[QUALITY], h))
    each(
        strip_n, me_s, lambda peer: peer,
        lambda peer: arrived(peer, carry_v.at[peer], cs_recv.at[peer], strip=peer),
    )
    carried = carry_v[0]
    for i in range(1, strip_n):
        carried = carried + carry_v[i]
    for i, h in enumerate(halves):
        j = len(halves) + i
        value = sums[i] + prefix_v[:, h] * carried[i : i + 1] + suffix_v[:, h] * carried[j : j + 1]
        value = value * scale_v[:, h]
        out_v[h, :] = value.T
        low_v[:, h] = value.astype(BF16)
    per = factors // strip_n
    act_v[...] = out_v[pl.ds(pl.multiple_of(me_s * per, per), per), :]

    @pl.when(me_s < strip_n - 1)
    def _():
        halo_copy(0).wait_send()

    @pl.when(me_s > 0)
    def _():
        halo_copy(1).wait_send()

    each(strip_n, me_s, rs_copy, lambda copy: copy.wait_send())
    each(tm_n, me_t, tm_copy, lambda copy: copy.wait_send())
    each(strip_n, me_s, ag_copy, lambda copy: copy.wait_send())
    each(strip_n, me_s, cs_copy, lambda copy: copy.wait_send())
    foot_load.wait()


def rebuild(low_v, warp_v, foot_v, act_v, act_h, res_h, res_v, sem):
    pixels = warp_v.shape[1]
    tile, wide = 512, 1024
    copies = [pltpu.make_async_copy(act_v, act_h, sem.at[0])]
    copies[0].start()
    low = low_v[...]
    for at in range(0, pixels, wide):
        for n in range(at, at + wide, tile):
            n = slice(n, n + tile)
            rebuilt = jnp.dot(low, foot_v[:, n], preferred_element_type=F32)
            res_v[:, n] = (warp_v[:, n].astype(F32) - rebuilt).astype(BF16)
        part = pl.ds(at, wide)
        copy = pltpu.make_async_copy(res_v.at[:, part], res_h.at[:, part], sem.at[1 + at // wide])
        copy.start()
        copies.append(copy)
    for copy in copies:
        copy.wait()


def body(tm_n, strip_n, movie, shifts, projection, footprints, quality, continuity, retention):
    frames, pixels = movie.shape
    factors = projection.shape[1]
    rows = shifts.shape[1]
    cols = pixels // rows
    per = factors // strip_n
    share = frames // strip_n
    halves = factors // 128
    steps = frames.bit_length() - 1
    DMA = pltpu.SemaphoreType.DMA
    vmem = pl.BlockSpec(memory_space=pltpu.VMEM)
    hbm = pl.BlockSpec(memory_space=pltpu.HBM)
    low, warped, foot, act = pl.pallas_call(
        functools.partial(kernel, tm_n, strip_n),
        out_shape=(
            pltpu.VMEM((frames, factors), BF16),
            pltpu.VMEM((frames, pixels), BF16),
            pltpu.VMEM((factors, pixels), BF16),
            pltpu.VMEM((per, frames), F32),
        ),
        in_specs=[hbm] * 7,
        out_specs=(vmem,) * 4,
        scratch_shapes=[
            pltpu.VMEM((frames, pixels), BF16),
            pltpu.VMEM((pixels, factors), BF16),
            pltpu.VMEM((2, frames, cols), BF16),
            pltpu.VMEM((rows, frames, 128), F32),
            pltpu.VMEM((rows, frames), F32),
            pltpu.VMEM((tm_n, frames), F32),
            pltpu.VMEM((tm_n, frames), F32),
            pltpu.VMEM((1, factors), F32),
            pltpu.VMEM((2 * steps + 4, frames, 128), F32),
            pltpu.VMEM((4, tm_n, frames), F32),
            pltpu.VMEM((frames, factors), F32),
            pltpu.VMEM((frames, factors), F32),
            pltpu.VMEM((frames, factors), F32),
            pltpu.VMEM((2 * halves, tm_n, 128), F32),
            pltpu.VMEM((frames, factors), F32),
            pltpu.VMEM((strip_n, share, factors), F32),
            pltpu.VMEM((frames, factors), F32),
            pltpu.VMEM((tm_n, 2 * halves, 128), F32),
            pltpu.VMEM((strip_n, 2 * halves, 128), F32),
            pltpu.VMEM((factors, frames), F32),
            DMA((7,)), DMA((2,)), DMA((2,)),
            DMA((strip_n,)), DMA((strip_n,)), DMA((tm_n,)), DMA((tm_n,)),
            DMA((strip_n,)), DMA((strip_n,)), DMA((strip_n,)), DMA((strip_n,)),
        ],
        compiler_params=pltpu.CompilerParams(
            collective_id=0, has_side_effects=True, vmem_limit_bytes=32 << 20
        ),
    )(
        *(
            pltpu.with_memory_space_constraint(x, pltpu.HBM)
            for x in (
                movie, shifts.T, projection, footprints,
                quality.reshape(tm_n, frames), continuity.reshape(tm_n, frames),
                retention.reshape(1, factors),
            )
        )
    )
    return pl.pallas_call(
        rebuild,
        out_shape=(
            jax.ShapeDtypeStruct((per, frames), F32),
            jax.ShapeDtypeStruct((frames, pixels), BF16),
        ),
        in_specs=[vmem] * 4,
        out_specs=(hbm, hbm),
        scratch_shapes=[pltpu.VMEM((frames, pixels), BF16), DMA((1 + pixels // 1024,))],
        compiler_params=pltpu.CompilerParams(vmem_limit_bytes=16 << 20),
    )(low, warped, foot, act)


def solution(mesh):
    return jax.shard_map(
        functools.partial(body, mesh.shape["tm"], mesh.shape["strip"]),
        mesh=mesh,
        in_specs=(
            P("tm", "strip"), P("tm", "strip"), P("strip", None), P(None, "strip"), P(), P(), P(),
        ),
        out_specs=(P("strip", "tm"), P("tm", "strip")),
        check_vma=False,
    )
```

time: 38.5 us -> 30.7 us (0.80)
  the two profiles are of different devices: /device:TPU:1 before, /device:TPU:6 now
where the time goes in v2:
time: 30.7 us
  Pallas kernels  30 us (98%)
  between operations  0.64 us (2%)
    pallas_call x1, Pallas kernels, body(): pl.pallas_call(functools.partial(kernel, tm_n, strip_n), out_shape=(pltpu...  28.4 us
    pallas_call x1, Pallas kernels, body(): pl.pallas_call(rebuild, out_shape=(jax.ShapeDtypeStruct((per, frames), F3...  1.63 us

profile of v2, /device:TPU:6, one launch (start us, length us, event | category | flops | bytes accessed | tf_op | source)
XLA Modules:
  0.0 30.7 jit_solution(7213194300081190580)
XLA Ops:
  0.6 28.4 %shard_map.86 = (bf16[128,256]{1,0:T(8,128)(2,1)S(1)}, bf16[128,8192]{1,0:T(8,128)(2,1)S(1)}, bf16[256,8192]{1,0:T(8,128)(2,1)S(1)}, f32[32,128]{1,0:T(8,128)S(1)}) custom-call(bf16[128,8192]{1,0:T(8,128)(2,1)} %movie_h.1, f32[16,128]{1,0:T(8,128)} %bitcast.6, bf16[8192,256]{1,0:T(8,128)(2,1)} %proj_h.1, bf16[256,8192]{1,0:T(8,128)(2,1)} %foot_h.1, ...), custom_call_target="tpu_custom_call" | custom-call | tf_op jit(solution)/shard_map/pallas_call | solution.py:394
  29.0 1.6 %shard_map.87 = (f32[32,128]{1,0:T(8,128)}, bf16[128,8192]{1,0:T(8,128)(2,1)}) custom-call(bf16[128,256]{1,0:T(8,128)(2,1)S(1)} %get-tuple-element.6.low_v, bf16[128,8192]{1,0:T(8,128)(2,1)S(1)} %get-tuple-element.7.warp_v, bf16[256,8192]{1,0:T(8,128)(2,1)S(1)} %get-tuple-element.8.foot_v, f32[32,128]{1,0:T(8,128)S(1)} %get-tuple-element.9.act_v), custom_call_target="tpu_custom_call" | custom-call | tf_op jit(solution)/shard_map/pallas_call | solution.py:442

commit v3 on v2

--- a/solution.py
+++ b/solution.py
@@ -11,6 +11,8 @@
 HI = lax.Precision.HIGHEST
 F32 = jnp.float32
 BF16 = jnp.bfloat16
+Z, CORES, Y = 8, 2, 4
+ROUNDS = 4
 
 
 def lane_shift(x, d, fill):
@@ -43,7 +45,7 @@
     col_v, rows_v, prefix_v, suffix_v, scale_v, coef_v, part_v,
     rs_v, all_v, tm_v, carry_v, out_v,
     load_sem, halo_send, halo_recv, rs_send, rs_recv, tm_send, tm_recv,
-    ag_send, ag_recv, cs_send, cs_recv,
+    ag_send, ag_recv, cs_send, cs_recv, ends_v, sent_v, round_sem,
 ):
     frames, pixels = movie_v.shape
     factors = proj_v.shape[1]
@@ -56,21 +58,39 @@
     halves = [slice(i, i + 128) for i in range(0, factors, 128)]
 
     barrier = pltpu.get_barrier_semaphore()
-
-    def hail_strip(d, _):
-        pl.semaphore_signal(
-            barrier, inc=1, device_id={"strip": lax.rem(me_s + d, strip_n)}, device_id_type=MESH
-        )
-        return 0
-
-    def hail_tm(d, _):
-        pl.semaphore_signal(
-            barrier, inc=1, device_id={"tm": lax.rem(me_t + d, tm_n)}, device_id_type=MESH
-        )
-        return 0
-
-    lax.fori_loop(1, strip_n, hail_strip, 0)
-    lax.fori_loop(1, tm_n, hail_tm, 0)
+    plane = Z * CORES
+    other_x = lax.rem(me_t + plane, 2 * plane)
+    flip = 1 - 2 * lax.rem(me_t, CORES)
+    corner = me_s // Y * Y
+    near = [
+        {"tm": other_x},
+        {"tm": other_x, "strip": lax.rem(me_s + Y, 2 * Y)},
+        {"strip": corner + lax.rem(me_s + 1, Y)},
+        {"strip": corner + lax.rem(me_s + Y - 1, Y)},
+        {"tm": me_t // plane * plane + lax.rem(me_t + CORES, plane)},
+        {"tm": me_t // plane * plane + lax.rem(me_t + plane - CORES, plane)},
+    ]
+    pair = [{"tm": me_t + flip}, {"tm": other_x + flip}]
+
+    def hail(sem, partners):
+        for partner in partners:
+            pl.semaphore_signal(sem, inc=1, device_id=partner, device_id_type=MESH)
+
+    @pl.when(me_s == Y - 1)
+    def _():
+        hail(barrier, [{"strip": Y}])
+
+    @pl.when(me_s == Y)
+    def _():
+        hail(barrier, [{"strip": Y - 1}])
+
+    hail(barrier, near + pair)
+
+    def next_round(n):
+        if n:
+            pl.semaphore_wait(round_sem.at[n - 1], len(near))
+        if n < ROUNDS:
+            hail(round_sem.at[n], near)
 
     small = [
         pltpu.make_async_copy(source, target, load_sem.at[i])
@@ -85,7 +105,15 @@
     foot_load = pltpu.make_async_copy(foot_h, foot_v, load_sem.at[6])
     for copy in small + large:
         copy.start()
-    pl.semaphore_wait(barrier, strip_n - 1 + tm_n - 1)
+    crossing = (me_s == Y - 1) | (me_s == Y)
+
+    @pl.when(crossing)
+    def _():
+        pl.semaphore_wait(barrier, len(near) + len(pair) + 1)
+
+    @pl.when(jnp.logical_not(crossing))
+    def _():
+        pl.semaphore_wait(barrier, len(near) + len(pair))
 
     def halo_copy(side):
         source = pl.ds((rows - 1) * cols, cols) if side == 0 else pl.ds(0, cols)
@@ -112,6 +140,7 @@
     def _():
         halo_v[1] = jnp.zeros((frames, cols), BF16)
 
+    next_round(0)
     for copy in small:
         copy.wait()
 
@@ -130,6 +159,7 @@
         prefix = prefix * lane_shift(prefix, d, 1.0)
         suffix = suffix * lane_shift(suffix, -d, 1.0)
     after = lane_shift(suffix, -1, 1.0)
+    next_round(1)
     rows_v[0] = quality
     rows_v[1] = cont
     rows_v[2] = prefix
@@ -184,6 +214,7 @@
         at = slice(first * cols, last * cols)
         return jnp.dot(warp_v[:, at], proj_v[at, :], preferred_element_type=F32)
 
+    next_round(2)
     for copy in large:
         copy.wait()
     group = 4
@@ -193,6 +224,8 @@
             warp_into(h, row_ref(h - 1), row_ref(h + 1))
         inner = project(first, last)
         part_v[...] = inner if first == 1 else part_v[...] + inner
+        if first == 1 + 2 * group:
+            next_round(3)
     foot_load.start()
 
     @pl.when(me_s > 0)
@@ -214,14 +247,15 @@
 
     def rs_copy(peer):
         return pltpu.make_async_remote_copy(
-            src_ref=part_v.at[pl.ds(pl.multiple_of(peer * share, share), share)],
+            src_ref=sent_v.at[pl.ds(pl.multiple_of(peer * share, share), share)],
             dst_ref=rs_v.at[me_s], send_sem=rs_send.at[peer], recv_sem=rs_recv.at[me_s],
             device_id={"strip": peer}, device_id_type=MESH,
         )
 
-    def tm_copy(peer):
+    def tm_copy(d):
+        peer = lax.rem(me_t + d, tm_n)
         return pltpu.make_async_remote_copy(
-            src_ref=tm_v.at[me_t], dst_ref=tm_v.at[me_t],
+            src_ref=ends_v.at[(me_t + d) // tm_n], dst_ref=tm_v.at[me_t],
             send_sem=tm_send.at[peer], recv_sem=tm_recv.at[me_t],
             device_id={"tm": peer}, device_id_type=MESH,
         )
@@ -241,6 +275,13 @@
             device_id={"strip": peer}, device_id_type=MESH,
         )
 
+    def each_d(count, act):
+        def one(d, _):
+            act(d)
+            return 0
+
+        lax.fori_loop(1, count, one, 0)
+
     def each(count, start, make, act):
         def one(d, _):
             act(make(lax.rem(start + d, count)))
@@ -248,13 +289,15 @@
 
         lax.fori_loop(1, count, one, 0)
 
+    sent_v[...] = part_v[...].astype(BF16)
     for i, h in enumerate(halves):
         weighted = part_v[:, h] * col_v[QUALITY]
-        tm_v[me_t, i : i + 1] = jnp.sum(weighted * suffix_v[:, h], axis=0, keepdims=True)
-        j = len(halves) + i
-        tm_v[me_t, j : j + 1] = jnp.sum(weighted * prefix_v[:, h], axis=0, keepdims=True)
+        ends_v[0, i : i + 1] = jnp.sum(weighted * suffix_v[:, h], axis=0, keepdims=True)
+        ends_v[1, i : i + 1] = jnp.sum(weighted * prefix_v[:, h], axis=0, keepdims=True)
+    tm_v[me_t] = jnp.zeros((len(halves), 128), F32)
     each(strip_n, me_s, rs_copy, lambda copy: copy.start())
-    each(tm_n, me_t, tm_copy, lambda copy: copy.start())
+    next_round(4)
+    each_d(tm_n, lambda d: tm_copy(d).start())
 
     def arrived(slot, ref, sem, **axis):
         pltpu.make_async_remote_copy(
@@ -285,15 +328,15 @@
         axis=0, keepdims=True,
     )
 
-    rs_v[me_s] = part_v[pl.ds(pl.multiple_of(me_s * share, share), share), :]
+    rs_v[me_s] = jnp.zeros((share, factors), BF16)
     each(
         strip_n, me_s, lambda peer: peer,
         lambda peer: arrived(peer, rs_v.at[peer], rs_recv.at[peer], strip=peer),
     )
-    total = rs_v[0]
-    for i in range(1, strip_n):
-        total = total + rs_v[i]
-    all_v[pl.ds(pl.multiple_of(me_s * share, share), share), :] = total
+    total = part_v[pl.ds(pl.multiple_of(me_s * share, share), share), :]
+    for i in range(strip_n):
+        total = total + rs_v[i].astype(F32)
+    all_v[pl.ds(pl.multiple_of(me_s * share, share), share), :] = total.astype(BF16)
     each(strip_n, me_s, ag_copy, lambda copy: copy.start())
 
     def smoothed(x, h):
@@ -315,9 +358,21 @@
         tm_n, me_t, lambda peer: peer,
         lambda peer: arrived(peer, tm_v.at[peer], tm_recv.at[peer], tm=peer),
     )
-    for i in range(2 * len(halves)):
-        carry_v[me_s, i : i + 1] = jnp.sum(coef_v[i] * tm_v[:, i, :], axis=0, keepdims=True)
+    for i in range(len(halves)):
+        for j in (i, len(halves) + i):
+            carry_v[me_s, j : j + 1] = jnp.sum(coef_v[j] * tm_v[:, i, :], axis=0, keepdims=True)
     each(strip_n, me_s, cs_copy, lambda copy: copy.start())
+
+    @pl.when(me_s < strip_n - 1)
+    def _():
+        halo_copy(0).wait_send()
+
+    @pl.when(me_s > 0)
+    def _():
+        halo_copy(1).wait_send()
+
+    each_d(tm_n, lambda d: tm_copy(d).wait_send())
+    each(strip_n, me_s, rs_copy, lambda copy: copy.wait_send())
 
     def share_of(peer):
         return all_v.at[pl.ds(pl.multiple_of(peer * share, share), share)]
@@ -328,7 +383,7 @@
     )
     sums = []
     for h in halves:
-        sums.append(smoothed(all_v[:, h] * col_v[QUALITY], h))
+        sums.append(smoothed(all_v[:, h].astype(F32) * col_v[QUALITY], h))
     each(
         strip_n, me_s, lambda peer: peer,
         lambda peer: arrived(peer, carry_v.at[peer], cs_recv.at[peer], strip=peer),
@@ -345,16 +400,6 @@
     per = factors // strip_n
     act_v[...] = out_v[pl.ds(pl.multiple_of(me_s * per, per), per), :]
 
-    @pl.when(me_s < strip_n - 1)
-    def _():
-        halo_copy(0).wait_send()
-
-    @pl.when(me_s > 0)
-    def _():
-        halo_copy(1).wait_send()
-
-    each(strip_n, me_s, rs_copy, lambda copy: copy.wait_send())
-    each(tm_n, me_t, tm_copy, lambda copy: copy.wait_send())
     each(strip_n, me_s, ag_copy, lambda copy: copy.wait_send())
     each(strip_n, me_s, cs_copy, lambda copy: copy.wait_send())
     foot_load.wait()
@@ -417,14 +462,17 @@
             pltpu.VMEM((frames, factors), F32),
             pltpu.VMEM((2 * halves, tm_n, 128), F32),
             pltpu.VMEM((frames, factors), F32),
-            pltpu.VMEM((strip_n, share, factors), F32),
-            pltpu.VMEM((frames, factors), F32),
-            pltpu.VMEM((tm_n, 2 * halves, 128), F32),
+            pltpu.VMEM((strip_n, share, factors), BF16),
+            pltpu.VMEM((frames, factors), BF16),
+            pltpu.VMEM((tm_n, halves, 128), F32),
             pltpu.VMEM((strip_n, 2 * halves, 128), F32),
             pltpu.VMEM((factors, frames), F32),
             DMA((7,)), DMA((2,)), DMA((2,)),
             DMA((strip_n,)), DMA((strip_n,)), DMA((tm_n,)), DMA((tm_n,)),
             DMA((strip_n,)), DMA((strip_n,)), DMA((strip_n,)), DMA((strip_n,)),
+            pltpu.VMEM((2, halves, 128), F32),
+            pltpu.VMEM((frames, factors), BF16),
+            pltpu.SemaphoreType.REGULAR((ROUNDS,)),
         ],
         compiler_params=pltpu.CompilerParams(
             collective_id=0, has_side_effects=True, vmem_limit_bytes=32 << 20

time: 30.7 us -> 29.5 us (0.961)
  the two profiles are of different devices: /device:TPU:6 before, /device:TPU:1 now
where the time goes in v3:
time: 29.5 us; the launch traced here: 29.4 us
  Pallas kernels  28.8 us (98%)
  between operations  0.64 us (2%)
    pallas_call x1, Pallas kernels, body(): pl.pallas_call(functools.partial(kernel, tm_n, strip_n), out_shape=(pltpu...  27.1 us
    pallas_call x1, Pallas kernels, body(): pl.pallas_call(rebuild, out_shape=(jax.ShapeDtypeStruct((per, frames), F3...  1.64 us

profile of v3, /device:TPU:1, one launch (start us, length us, event | category | flops | bytes accessed | tf_op | source)
XLA Modules:
  0.0 29.4 jit_solution(17198678664029163509)
XLA Ops:
  0.6 27.1 %shard_map.86 = (bf16[128,256]{1,0:T(8,128)(2,1)S(1)}, bf16[128,8192]{1,0:T(8,128)(2,1)S(1)}, bf16[256,8192]{1,0:T(8,128)(2,1)S(1)}, f32[32,128]{1,0:T(8,128)S(1)}) custom-call(bf16[128,8192]{1,0:T(8,128)(2,1)} %movie_h.1, f32[16,128]{1,0:T(8,128)} %bitcast.6, bf16[8192,256]{1,0:T(8,128)(2,1)} %proj_h.1, bf16[256,8192]{1,0:T(8,128)(2,1)} %foot_h.1, ...), custom_call_target="tpu_custom_call" | custom-call | tf_op jit(solution)/shard_map/pallas_call | solution.py:439
  27.8 1.6 %shard_map.87 = (f32[32,128]{1,0:T(8,128)}, bf16[128,8192]{1,0:T(8,128)(2,1)}) custom-call(bf16[128,256]{1,0:T(8,128)(2,1)S(1)} %get-tuple-element.6.low_v, bf16[128,8192]{1,0:T(8,128)(2,1)S(1)} %get-tuple-element.7.warp_v, bf16[256,8192]{1,0:T(8,128)(2,1)S(1)} %get-tuple-element.8.foot_v, f32[32,128]{1,0:T(8,128)S(1)} %get-tuple-element.9.act_v), custom_call_target="tpu_custom_call" | custom-call | tf_op jit(solution)/shard_map/pallas_call | solution.py:490

commit v4 on v3

--- a/solution.py
+++ b/solution.py
@@ -12,7 +12,7 @@
 F32 = jnp.float32
 BF16 = jnp.bfloat16
 Z, CORES, Y = 8, 2, 4
-ROUNDS = 4
+ROUNDS = 3
 
 
 def lane_shift(x, d, fill):
@@ -44,8 +44,7 @@
     movie_v, proj_v, halo_v, shift_v, shifts_r, quality_r, cont_r, ret_r,
     col_v, rows_v, prefix_v, suffix_v, scale_v, coef_v, part_v,
     rs_v, all_v, tm_v, carry_v, out_v,
-    load_sem, halo_send, halo_recv, rs_send, rs_recv, tm_send, tm_recv,
-    ag_send, ag_recv, cs_send, cs_recv, ends_v, sent_v, round_sem,
+    load_sem, halo_send, halo_recv, sems, ends_v, sent_v, enter_v, table_v, round_sem,
 ):
     frames, pixels = movie_v.shape
     factors = proj_v.shape[1]
@@ -62,6 +61,8 @@
     other_x = lax.rem(me_t + plane, 2 * plane)
     flip = 1 - 2 * lax.rem(me_t, CORES)
     corner = me_s // Y * Y
+    planes = [me_t, other_x]
+    place = lax.rem(me_t, plane)
     near = [
         {"tm": other_x},
         {"tm": other_x, "strip": lax.rem(me_s + Y, 2 * Y)},
@@ -70,7 +71,7 @@
         {"tm": me_t // plane * plane + lax.rem(me_t + CORES, plane)},
         {"tm": me_t // plane * plane + lax.rem(me_t + plane - CORES, plane)},
     ]
-    pair = [{"tm": me_t + flip}, {"tm": other_x + flip}]
+    pair = [{"tm": me_t + flip}] + [{"tm": one["tm"] + flip} for one in near[4:]]
 
     def hail(sem, partners):
         for partner in partners:
@@ -248,39 +249,40 @@
     def rs_copy(peer):
         return pltpu.make_async_remote_copy(
             src_ref=sent_v.at[pl.ds(pl.multiple_of(peer * share, share), share)],
-            dst_ref=rs_v.at[me_s], send_sem=rs_send.at[peer], recv_sem=rs_recv.at[me_s],
+            dst_ref=rs_v.at[me_s], send_sem=sems.at[0], recv_sem=sems.at[1],
             device_id={"strip": peer}, device_id_type=MESH,
         )
 
-    def tm_copy(d):
-        peer = lax.rem(me_t + d, tm_n)
+    def tm_copy(peer):
         return pltpu.make_async_remote_copy(
-            src_ref=ends_v.at[(me_t + d) // tm_n], dst_ref=tm_v.at[me_t],
-            send_sem=tm_send.at[peer], recv_sem=tm_recv.at[me_t],
-            device_id={"tm": peer}, device_id_type=MESH,
+            src_ref=ends_v, dst_ref=tm_v.at[place], send_sem=sems.at[2], recv_sem=sems.at[3],
+            device_id={"tm": me_t // plane * plane + peer}, device_id_type=MESH,
         )
 
     def ag_copy(peer):
         mine = pl.ds(pl.multiple_of(me_s * share, share), share)
         return pltpu.make_async_remote_copy(
             src_ref=all_v.at[mine], dst_ref=all_v.at[mine],
-            send_sem=ag_send.at[peer], recv_sem=ag_recv.at[me_s],
+            send_sem=sems.at[4], recv_sem=sems.at[5],
             device_id={"strip": peer}, device_id_type=MESH,
         )
 
-    def cs_copy(peer):
+    def cs_copy(j, peer):
+        slot = j * strip_n + me_s
         return pltpu.make_async_remote_copy(
-            src_ref=carry_v.at[me_s], dst_ref=carry_v.at[me_s],
-            send_sem=cs_send.at[peer], recv_sem=cs_recv.at[me_s],
-            device_id={"strip": peer}, device_id_type=MESH,
-        )
-
-    def each_d(count, act):
-        def one(d, _):
-            act(d)
-            return 0
-
-        lax.fori_loop(1, count, one, 0)
+            src_ref=enter_v.at[j], dst_ref=carry_v.at[slot],
+            send_sem=sems.at[6], recv_sem=sems.at[7],
+            device_id={"tm": planes[j], "strip": peer}, device_id_type=MESH,
+        )
+
+    def each_cs(act):
+        for j in range(len(planes)):
+
+            def one(d, _):
+                act(j, lax.rem(me_s + d, strip_n))
+                return 0
+
+            lax.fori_loop(1 if j == 0 else 0, strip_n, one, 0)
 
     def each(count, start, make, act):
         def one(d, _):
@@ -292,53 +294,62 @@
     sent_v[...] = part_v[...].astype(BF16)
     for i, h in enumerate(halves):
         weighted = part_v[:, h] * col_v[QUALITY]
-        ends_v[0, i : i + 1] = jnp.sum(weighted * suffix_v[:, h], axis=0, keepdims=True)
-        ends_v[1, i : i + 1] = jnp.sum(weighted * prefix_v[:, h], axis=0, keepdims=True)
-    tm_v[me_t] = jnp.zeros((len(halves), 128), F32)
+        j = len(halves) + i
+        ends_v[i : i + 1] = jnp.sum(weighted * suffix_v[:, h], axis=0, keepdims=True)
+        ends_v[j : j + 1] = jnp.sum(weighted * prefix_v[:, h], axis=0, keepdims=True)
+    tm_v[place] = ends_v[...]
     each(strip_n, me_s, rs_copy, lambda copy: copy.start())
-    next_round(4)
-    each_d(tm_n, lambda d: tm_copy(d).start())
-
-    def arrived(slot, ref, sem, **axis):
-        pltpu.make_async_remote_copy(
-            src_ref=ref, dst_ref=ref, send_sem=sem, recv_sem=sem,
-            device_id=axis, device_id_type=MESH,
-        ).wait_recv()
+    each(plane, place, tm_copy, lambda copy: copy.start())
+
+    def settled(ref, count, i):
+        part = ref.at[pl.ds(0, count)]
+        pltpu.make_async_copy(part, part, sems.at[i]).wait()
 
     whole = prefix[:, frames - 1 : frames] * powers[steps]
     block = lax.broadcasted_iota(jnp.int32, (tm_n, factors), 0)
-    before = jnp.where(block < me_t, whole, 1.0)
-    beyond = jnp.where(block > me_t, whole, 1.0)
-    d = 1
-    while d < tm_n:
-        before = before * row_shift(before, -d, 1.0)
-        beyond = beyond * row_shift(beyond, d, 1.0)
-        d *= 2
-    before = jnp.where(block < me_t, row_shift(before, -1, 1.0), 0.0)
-    beyond = jnp.where(block > me_t, row_shift(beyond, 1, 1.0), 0.0)
-    for i, h in enumerate(halves):
-        coef_v[i] = before[:, h]
-        coef_v[len(halves) + i] = beyond[:, h]
-    norm_in = jnp.sum(
-        before * jnp.dot(quality * after, falling, precision=HI, preferred_element_type=F32),
-        axis=0, keepdims=True,
-    )
-    norm_out = jnp.sum(
-        beyond * jnp.dot(quality * prefix, rising, precision=HI, preferred_element_type=F32),
-        axis=0, keepdims=True,
-    )
+    mine = pl.ds(pl.multiple_of(me_t // plane * plane, plane), plane)
+    for j, target in enumerate(planes):
+        before = jnp.where(block < target, whole, 1.0)
+        beyond = jnp.where(block > target, whole, 1.0)
+        d = 1
+        while d < tm_n:
+            before = before * row_shift(before, -d, 1.0)
+            beyond = beyond * row_shift(beyond, d, 1.0)
+            d *= 2
+        before = jnp.where(block < target, row_shift(before, -1, 1.0), 0.0)
+        beyond = jnp.where(block > target, row_shift(beyond, 1, 1.0), 0.0)
+        for i, h in enumerate(halves):
+            table_v[i] = before[:, h]
+            table_v[len(halves) + i] = beyond[:, h]
+        for i in range(2 * len(halves)):
+            coef_v[j, i] = table_v[i, mine, :]
+        if j == 0:
+            norm_in = jnp.sum(
+                before
+                * jnp.dot(quality * after, falling, precision=HI, preferred_element_type=F32),
+                axis=0, keepdims=True,
+            )
+            norm_out = jnp.sum(
+                beyond
+                * jnp.dot(quality * prefix, rising, precision=HI, preferred_element_type=F32),
+                axis=0, keepdims=True,
+            )
 
     rs_v[me_s] = jnp.zeros((share, factors), BF16)
-    each(
-        strip_n, me_s, lambda peer: peer,
-        lambda peer: arrived(peer, rs_v.at[peer], rs_recv.at[peer], strip=peer),
-    )
+    settled(rs_v, strip_n - 1, 1)
     total = part_v[pl.ds(pl.multiple_of(me_s * share, share), share), :]
     for i in range(strip_n):
         total = total + rs_v[i].astype(F32)
     all_v[pl.ds(pl.multiple_of(me_s * share, share), share), :] = total.astype(BF16)
     each(strip_n, me_s, ag_copy, lambda copy: copy.start())
 
+    settled(tm_v, plane - 1, 3)
+    for i in range(2 * len(halves)):
+        ends = tm_v[:, i, :]
+        for j in range(len(planes)):
+            enter_v[j, i : i + 1] = jnp.sum(coef_v[j, i] * ends, axis=0, keepdims=True)
+    carry_v[me_s] = enter_v[0]
+    each_cs(lambda j, peer: cs_copy(j, peer).start())
     def smoothed(x, h):
         fore = x
         back = x * (col_v[CONT] * ret[:, h])
@@ -354,15 +365,6 @@
         norm = norm + prefix_v[:, h] * norm_in[:, h] + suffix_v[:, h] * norm_out[:, h]
         scale_v[:, h] = 1.0 / jnp.sqrt(norm)
 
-    each(
-        tm_n, me_t, lambda peer: peer,
-        lambda peer: arrived(peer, tm_v.at[peer], tm_recv.at[peer], tm=peer),
-    )
-    for i in range(len(halves)):
-        for j in (i, len(halves) + i):
-            carry_v[me_s, j : j + 1] = jnp.sum(coef_v[j] * tm_v[:, i, :], axis=0, keepdims=True)
-    each(strip_n, me_s, cs_copy, lambda copy: copy.start())
-
     @pl.when(me_s < strip_n - 1)
     def _():
         halo_copy(0).wait_send()
@@ -371,25 +373,17 @@
     def _():
         halo_copy(1).wait_send()
 
-    each_d(tm_n, lambda d: tm_copy(d).wait_send())
-    each(strip_n, me_s, rs_copy, lambda copy: copy.wait_send())
-
-    def share_of(peer):
-        return all_v.at[pl.ds(pl.multiple_of(peer * share, share), share)]
-
-    each(
-        strip_n, me_s, lambda peer: peer,
-        lambda peer: arrived(peer, share_of(peer), ag_recv.at[peer], strip=peer),
-    )
+    settled(rs_v, strip_n - 1, 0)
+    settled(tm_v, plane - 1, 2)
+    settled(carry_v, len(planes) * strip_n - 1, 6)
+    foot_load.wait()
+    settled(all_v, (strip_n - 1) * share, 5)
     sums = []
     for h in halves:
         sums.append(smoothed(all_v[:, h].astype(F32) * col_v[QUALITY], h))
-    each(
-        strip_n, me_s, lambda peer: peer,
-        lambda peer: arrived(peer, carry_v.at[peer], cs_recv.at[peer], strip=peer),
-    )
+    settled(carry_v, len(planes) * strip_n - 1, 7)
     carried = carry_v[0]
-    for i in range(1, strip_n):
+    for i in range(1, len(planes) * strip_n):
         carried = carried + carry_v[i]
     for i, h in enumerate(halves):
         j = len(halves) + i
@@ -400,9 +394,7 @@
     per = factors // strip_n
     act_v[...] = out_v[pl.ds(pl.multiple_of(me_s * per, per), per), :]
 
-    each(strip_n, me_s, ag_copy, lambda copy: copy.wait_send())
-    each(strip_n, me_s, cs_copy, lambda copy: copy.wait_send())
-    foot_load.wait()
+    settled(all_v, (strip_n - 1) * share, 4)
 
 
 def rebuild(low_v, warp_v, foot_v, act_v, act_h, res_h, res_v, sem):
@@ -460,18 +452,19 @@
             pltpu.VMEM((frames, factors), F32),
             pltpu.VMEM((frames, factors), F32),
             pltpu.VMEM((frames, factors), F32),
-            pltpu.VMEM((2 * halves, tm_n, 128), F32),
+            pltpu.VMEM((2, 2 * halves, Z * CORES, 128), F32),
             pltpu.VMEM((frames, factors), F32),
             pltpu.VMEM((strip_n, share, factors), BF16),
             pltpu.VMEM((frames, factors), BF16),
-            pltpu.VMEM((tm_n, halves, 128), F32),
-            pltpu.VMEM((strip_n, 2 * halves, 128), F32),
+            pltpu.VMEM((Z * CORES, 2 * halves, 128), F32),
+            pltpu.VMEM((2 * strip_n, 2 * halves, 128), F32),
             pltpu.VMEM((factors, frames), F32),
             DMA((7,)), DMA((2,)), DMA((2,)),
-            DMA((strip_n,)), DMA((strip_n,)), DMA((tm_n,)), DMA((tm_n,)),
-            DMA((strip_n,)), DMA((strip_n,)), DMA((strip_n,)), DMA((strip_n,)),
-            pltpu.VMEM((2, halves, 128), F32),
+            DMA((8,)),
+            pltpu.VMEM((2 * halves, 128), F32),
             pltpu.VMEM((frames, factors), BF16),
+            pltpu.VMEM((2, 2 * halves, 128), F32),
+            pltpu.VMEM((2 * halves, tm_n, 128), F32),
             pltpu.SemaphoreType.REGULAR((ROUNDS,)),
         ],
         compiler_params=pltpu.CompilerParams(

time: 29.5 us -> 27.5 us (0.932)
  Pallas kernels: 28.8 us -> 26.8 us
    pallas_call x1, Pallas kernels: 27.1 us -> 25.1 us  [body(): pl.pallas_call(functools.partial(kernel, tm_n, strip_n), out_shape=(pltpu...]
where the time goes in v4:
time: 27.5 us; the launch traced here: 27.4 us
  Pallas kernels  26.8 us (97%)
  between operations  0.64 us (2%)
    pallas_call x1, Pallas kernels, body(): pl.pallas_call(functools.partial(kernel, tm_n, strip_n), out_shape=(pltpu...  25.1 us
    pallas_call x1, Pallas kernels, body(): pl.pallas_call(rebuild, out_shape=(jax.ShapeDtypeStruct((per, frames), F3...  1.63 us

profile of v4, /device:TPU:1, one launch (start us, length us, event | category | flops | bytes accessed | tf_op | source)
XLA Modules:
  0.0 27.4 jit_solution(13430279185356973)
XLA Ops:
  0.6 25.1 %shard_map.86 = (bf16[128,256]{1,0:T(8,128)(2,1)S(1)}, bf16[128,8192]{1,0:T(8,128)(2,1)S(1)}, bf16[256,8192]{1,0:T(8,128)(2,1)S(1)}, f32[32,128]{1,0:T(8,128)S(1)}) custom-call(bf16[128,8192]{1,0:T(8,128)(2,1)} %movie_h.1, f32[16,128]{1,0:T(8,128)} %bitcast.6, bf16[8192,256]{1,0:T(8,128)(2,1)} %proj_h.1, bf16[256,8192]{1,0:T(8,128)(2,1)} %foot_h.1, ...), custom_call_target="tpu_custom_call" | custom-call | tf_op jit(solution)/shard_map/pallas_call | solution.py:431
  25.8 1.6 %shard_map.87 = (f32[32,128]{1,0:T(8,128)}, bf16[128,8192]{1,0:T(8,128)(2,1)}) custom-call(bf16[128,256]{1,0:T(8,128)(2,1)S(1)} %get-tuple-element.6.low_v, bf16[128,8192]{1,0:T(8,128)(2,1)S(1)} %get-tuple-element.7.warp_v, bf16[256,8192]{1,0:T(8,128)(2,1)S(1)} %get-tuple-element.8.foot_v, f32[32,128]{1,0:T(8,128)S(1)} %get-tuple-element.9.act_v), custom_call_target="tpu_custom_call" | custom-call | tf_op jit(solution)/shard_map/pallas_call | solution.py:483

commit v5 on v4

--- a/solution.py
+++ b/solution.py
@@ -229,19 +229,35 @@
             next_round(3)
     foot_load.start()
 
-    @pl.when(me_s > 0)
-    def _():
-        halo_copy(0).wait_recv()
-
-    warp_into(0, halo_v.at[0], row_ref(1))
-    part_v[...] += project(0, 1)
-
-    @pl.when(me_s < strip_n - 1)
-    def _():
-        halo_copy(1).wait_recv()
-
-    warp_into(rows - 1, row_ref(rows - 2), halo_v.at[1])
-    part_v[...] += project(rows - 1, rows)
+    swap = me_s // Y - me_s // (Y + 1)
+
+    def edge(n, _):
+        side = lax.rem(n + swap, 2)
+
+        @pl.when(me_s + side * (strip_n - 1) - me_s * side * 2 > 0)
+        def _():
+            pltpu.make_async_copy(halo_v.at[side], halo_v.at[side], halo_recv.at[side]).wait()
+
+        at = pl.multiple_of(side * (rows - 1) * cols, cols)
+        inner = pl.multiple_of((1 + side * (rows - 3)) * cols, cols)
+        s = shift_v[side * (rows - 1)]
+        near_weight = jnp.abs(s)
+        keep = jnp.maximum(0.0, 1.0 - near_weight)
+        outside = s * (2 * side - 1).astype(F32) > 0.0
+        for w in range(0, cols, 128):
+            other = jnp.where(
+                outside,
+                halo_v[side, :, w : w + 128].astype(F32),
+                movie_v[:, pl.ds(inner + w, 128)].astype(F32),
+            )
+            own = movie_v[:, pl.ds(at + w, 128)].astype(F32)
+            warp_v[:, pl.ds(at + w, 128)] = (keep * own + near_weight * other).astype(BF16)
+        part_v[...] += jnp.dot(
+            warp_v[:, pl.ds(at, cols)], proj_v[pl.ds(at, cols), :], preferred_element_type=F32
+        )
+        return 0
+
+    lax.fori_loop(0, 2, edge, 0)
 
     def strip_peer(d):
         return lax.rem(me_s + d, strip_n)
@@ -275,31 +291,24 @@
             device_id={"tm": planes[j], "strip": peer}, device_id_type=MESH,
         )
 
-    def each_cs(act):
-        for j in range(len(planes)):
-
-            def one(d, _):
-                act(j, lax.rem(me_s + d, strip_n))
-                return 0
-
-            lax.fori_loop(1 if j == 0 else 0, strip_n, one, 0)
-
-    def each(count, start, make, act):
-        def one(d, _):
-            act(make(lax.rem(start + d, count)))
-            return 0
-
-        lax.fori_loop(1, count, one, 0)
-
-    sent_v[...] = part_v[...].astype(BF16)
     for i, h in enumerate(halves):
         weighted = part_v[:, h] * col_v[QUALITY]
         j = len(halves) + i
         ends_v[i : i + 1] = jnp.sum(weighted * suffix_v[:, h], axis=0, keepdims=True)
         ends_v[j : j + 1] = jnp.sum(weighted * prefix_v[:, h], axis=0, keepdims=True)
     tm_v[place] = ends_v[...]
-    each(strip_n, me_s, rs_copy, lambda copy: copy.start())
-    each(plane, place, tm_copy, lambda copy: copy.start())
+    for dz in (4, 3, 5, 2, 6, 1, 7, 0):
+        for dc in (1, 0):
+            if dz or dc:
+                other = lax.rem(place // CORES + dz, Z) * CORES + lax.rem(place + dc, CORES)
+                tm_copy(other).start()
+    sent_v[...] = part_v[...].astype(BF16)
+    peers = [
+        lax.rem(me_s // Y + dx, 2) * Y + lax.rem(me_s + dy, Y)
+        for dx, dy in ((1, 2), (1, 1), (1, 3), (0, 2), (1, 0), (0, 1), (0, 3))
+    ]
+    for peer in peers:
+        rs_copy(peer).start()
 
     def settled(ref, count, i):
         part = ref.at[pl.ds(0, count)]
@@ -341,7 +350,8 @@
     for i in range(strip_n):
         total = total + rs_v[i].astype(F32)
     all_v[pl.ds(pl.multiple_of(me_s * share, share), share), :] = total.astype(BF16)
-    each(strip_n, me_s, ag_copy, lambda copy: copy.start())
+    for peer in peers:
+        ag_copy(peer).start()
 
     settled(tm_v, plane - 1, 3)
     for i in range(2 * len(halves)):
@@ -349,7 +359,9 @@
         for j in range(len(planes)):
             enter_v[j, i : i + 1] = jnp.sum(coef_v[j, i] * ends, axis=0, keepdims=True)
     carry_v[me_s] = enter_v[0]
-    each_cs(lambda j, peer: cs_copy(j, peer).start())
+    for j in (1, 0):
+        for peer in peers + [me_s] * j:
+            cs_copy(j, peer).start()
     def smoothed(x, h):
         fore = x
         back = x * (col_v[CONT] * ret[:, h])
@@ -399,7 +411,7 @@
 
 def rebuild(low_v, warp_v, foot_v, act_v, act_h, res_h, res_v, sem):
     pixels = warp_v.shape[1]
-    tile, wide = 512, 1024
+    tile, wide = 512, 512
     copies = [pltpu.make_async_copy(act_v, act_h, sem.at[0])]
     copies[0].start()
     low = low_v[...]
@@ -488,7 +500,7 @@
         ),
         in_specs=[vmem] * 4,
         out_specs=(hbm, hbm),
-        scratch_shapes=[pltpu.VMEM((frames, pixels), BF16), DMA((1 + pixels // 1024,))],
+        scratch_shapes=[pltpu.VMEM((frames, pixels), BF16), DMA((1 + pixels // 512,))],
         compiler_params=pltpu.CompilerParams(vmem_limit_bytes=16 << 20),
     )(low, warped, foot, act)
 

time: 27.5 us -> 26.9 us (0.978)
  Pallas kernels: 26.8 us -> 26.2 us
    pallas_call x1, Pallas kernels: 25.1 us -> 24.5 us  [body(): pl.pallas_call(functools.partial(kernel, tm_n, strip_n), out_shape=(pltpu...]
where the time goes in v5:
time: 26.9 us; the launch traced here: 26.8 us
  Pallas kernels  26.2 us (97%)
  between operations  0.64 us (2%)
    pallas_call x1, Pallas kernels, body(): pl.pallas_call(functools.partial(kernel, tm_n, strip_n), out_shape=(pltpu...  24.5 us
    pallas_call x1, Pallas kernels, body(): pl.pallas_call(rebuild, out_shape=(jax.ShapeDtypeStruct((per, frames), F3...  1.66 us

profile of v5, /device:TPU:1, one launch (start us, length us, event | category | flops | bytes accessed | tf_op | source)
XLA Modules:
  0.0 26.8 jit_solution(13833693622667415408)
XLA Ops:
  0.6 24.5 %shard_map.86 = (bf16[128,256]{1,0:T(8,128)(2,1)S(1)}, bf16[128,8192]{1,0:T(8,128)(2,1)S(1)}, bf16[256,8192]{1,0:T(8,128)(2,1)S(1)}, f32[32,128]{1,0:T(8,128)S(1)}) custom-call(bf16[128,8192]{1,0:T(8,128)(2,1)} %movie_h.1, f32[16,128]{1,0:T(8,128)} %bitcast.6, bf16[8192,256]{1,0:T(8,128)(2,1)} %proj_h.1, bf16[256,8192]{1,0:T(8,128)(2,1)} %foot_h.1, ...), custom_call_target="tpu_custom_call" | custom-call | tf_op jit(solution)/shard_map/pallas_call | solution.py:443
  25.1 1.7 %shard_map.87 = (f32[32,128]{1,0:T(8,128)}, bf16[128,8192]{1,0:T(8,128)(2,1)}) custom-call(bf16[128,256]{1,0:T(8,128)(2,1)S(1)} %get-tuple-element.6.low_v, bf16[128,8192]{1,0:T(8,128)(2,1)S(1)} %get-tuple-element.7.warp_v, bf16[256,8192]{1,0:T(8,128)(2,1)S(1)} %get-tuple-element.8.foot_v, f32[32,128]{1,0:T(8,128)S(1)} %get-tuple-element.9.act_v), custom_call_target="tpu_custom_call" | custom-call | tf_op jit(solution)/shard_map/pallas_call | solution.py:495

commit v6 on v5

--- a/solution.py
+++ b/solution.py
@@ -43,7 +43,7 @@
     low_v, warp_v, foot_v, act_v,
     movie_v, proj_v, halo_v, shift_v, shifts_r, quality_r, cont_r, ret_r,
     col_v, rows_v, prefix_v, suffix_v, scale_v, coef_v, part_v,
-    rs_v, all_v, tm_v, carry_v, out_v,
+    rs_v, all_v, tm_v, carry_v,
     load_sem, halo_send, halo_recv, sems, ends_v, sent_v, enter_v, table_v, round_sem,
 ):
     frames, pixels = movie_v.shape
@@ -99,13 +99,21 @@
             ((shifts_h, shifts_r), (quality_h, quality_r), (cont_h, cont_r), (ret_h, ret_r))
         )
     ]
+    top, bottom = pl.ds(0, cols), pl.ds((rows - 1) * cols, cols)
+    middle = pl.ds(cols, (rows - 2) * cols)
+    edges = [
+        pltpu.make_async_copy(movie_h.at[:, part], movie_v.at[:, part], load_sem.at[i])
+        for i, part in ((7, top), (8, bottom))
+    ]
     large = [
-        pltpu.make_async_copy(movie_h, movie_v, load_sem.at[4]),
+        pltpu.make_async_copy(movie_h.at[:, middle], movie_v.at[:, middle], load_sem.at[4]),
         pltpu.make_async_copy(proj_h, proj_v, load_sem.at[5]),
     ]
     foot_load = pltpu.make_async_copy(foot_h, foot_v, load_sem.at[6])
-    for copy in small + large:
+    for copy in edges + small + large:
         copy.start()
+    for copy in edges:
+        copy.wait()
     crossing = (me_s == Y - 1) | (me_s == Y)
 
     @pl.when(crossing)
@@ -117,10 +125,10 @@
         pl.semaphore_wait(barrier, len(near) + len(pair))
 
     def halo_copy(side):
-        source = pl.ds((rows - 1) * cols, cols) if side == 0 else pl.ds(0, cols)
+        source = bottom if side == 0 else top
         target = me_s + 1 if side == 0 else me_s - 1
         return pltpu.make_async_remote_copy(
-            src_ref=movie_h.at[:, source], dst_ref=halo_v.at[side],
+            src_ref=movie_v.at[:, source], dst_ref=halo_v.at[side],
             send_sem=halo_send.at[side], recv_sem=halo_recv.at[side],
             device_id={"strip": target}, device_id_type=MESH,
         )
@@ -297,16 +305,19 @@
         ends_v[i : i + 1] = jnp.sum(weighted * suffix_v[:, h], axis=0, keepdims=True)
         ends_v[j : j + 1] = jnp.sum(weighted * prefix_v[:, h], axis=0, keepdims=True)
     tm_v[place] = ends_v[...]
+    here_z, here_c = lax.div(place, CORES), lax.rem(place, CORES)
     for dz in (4, 3, 5, 2, 6, 1, 7, 0):
-        for dc in (1, 0):
-            if dz or dc:
-                other = lax.rem(place // CORES + dz, Z) * CORES + lax.rem(place + dc, CORES)
-                tm_copy(other).start()
-    sent_v[...] = part_v[...].astype(BF16)
+        floor = lax.rem(here_z + dz, Z) * CORES
+        for core in (1 - here_c, here_c)[: 2 if dz else 1]:
+            tm_copy(floor + core).start()
+    across = lax.rem(me_s + Y, 2 * Y)
+    corners = [lax.div(one, Y) * Y for one in (me_s, across)]
+    ys = [lax.rem(me_s + dy, Y) for dy in range(Y)]
     peers = [
-        lax.rem(me_s // Y + dx, 2) * Y + lax.rem(me_s + dy, Y)
+        corners[dx] + ys[dy]
         for dx, dy in ((1, 2), (1, 1), (1, 3), (0, 2), (1, 0), (0, 1), (0, 3))
     ]
+    sent_v[...] = part_v[...].astype(BF16)
     for peer in peers:
         rs_copy(peer).start()
 
@@ -401,19 +412,16 @@
         j = len(halves) + i
         value = sums[i] + prefix_v[:, h] * carried[i : i + 1] + suffix_v[:, h] * carried[j : j + 1]
         value = value * scale_v[:, h]
-        out_v[h, :] = value.T
+        act_v[:, h] = value
         low_v[:, h] = value.astype(BF16)
-    per = factors // strip_n
-    act_v[...] = out_v[pl.ds(pl.multiple_of(me_s * per, per), per), :]
 
     settled(all_v, (strip_n - 1) * share, 4)
 
 
-def rebuild(low_v, warp_v, foot_v, act_v, act_h, res_h, res_v, sem):
+def rebuild(low_v, warp_v, foot_v, act_v, act_h, res_h, res_v, turned_v, sem):
     pixels = warp_v.shape[1]
     tile, wide = 512, 512
-    copies = [pltpu.make_async_copy(act_v, act_h, sem.at[0])]
-    copies[0].start()
+    copies = []
     low = low_v[...]
     for at in range(0, pixels, wide):
         for n in range(at, at + wide, tile):
@@ -424,6 +432,13 @@
         copy = pltpu.make_async_copy(res_v.at[:, part], res_h.at[:, part], sem.at[1 + at // wide])
         copy.start()
         copies.append(copy)
+        if at == 4 * wide:
+            per = act_h.shape[0]
+            for at in range(0, act_v.shape[1], 128):
+                turned_v[at : at + 128] = act_v[:, at : at + 128].T
+            mine = pl.ds(pl.multiple_of(lax.axis_index("strip") * per, per), per)
+            copies.append(pltpu.make_async_copy(turned_v.at[mine], act_h, sem.at[0]))
+            copies[-1].start()
     for copy in copies:
         copy.wait()
 
@@ -446,7 +461,7 @@
             pltpu.VMEM((frames, factors), BF16),
             pltpu.VMEM((frames, pixels), BF16),
             pltpu.VMEM((factors, pixels), BF16),
-            pltpu.VMEM((per, frames), F32),
+            pltpu.VMEM((frames, factors), F32),
         ),
         in_specs=[hbm] * 7,
         out_specs=(vmem,) * 4,
@@ -470,8 +485,7 @@
             pltpu.VMEM((frames, factors), BF16),
             pltpu.VMEM((Z * CORES, 2 * halves, 128), F32),
             pltpu.VMEM((2 * strip_n, 2 * halves, 128), F32),
-            pltpu.VMEM((factors, frames), F32),
-            DMA((7,)), DMA((2,)), DMA((2,)),
+            DMA((9,)), DMA((2,)), DMA((2,)),
             DMA((8,)),
             pltpu.VMEM((2 * halves, 128), F32),
             pltpu.VMEM((frames, factors), BF16),
@@ -500,7 +514,11 @@
         ),
         in_specs=[vmem] * 4,
         out_specs=(hbm, hbm),
-        scratch_shapes=[pltpu.VMEM((frames, pixels), BF16), DMA((1 + pixels // 512,))],
+        scratch_shapes=[
+            pltpu.VMEM((frames, pixels), BF16),
+            pltpu.VMEM((factors, frames), F32),
+            DMA((1 + pixels // 512,)),
+        ],
         compiler_params=pltpu.CompilerParams(vmem_limit_bytes=16 << 20),
     )(low, warped, foot, act)
 

time: 26.9 us -> 26.8 us (level)
  no operation moved by 1% of the time
where the time goes in v6:
time: 26.8 us
  Pallas kernels  26.1 us (97%)
  between operations  0.64 us (2%)
    pallas_call x1, Pallas kernels, body(): pl.pallas_call(functools.partial(kernel, tm_n, strip_n), out_shape=(pltpu...  24.4 us
    pallas_call x1, Pallas kernels, body(): pl.pallas_call(rebuild, out_shape=(jax.ShapeDtypeStruct((per, frames), F3...  1.67 us

profile of v6, /device:TPU:1, one launch (start us, length us, event | category | flops | bytes accessed | tf_op | source)
XLA Modules:
  0.0 26.8 jit_solution(6047045728933630588)
XLA Ops:
  0.6 24.4 %shard_map.86 = (bf16[128,256]{1,0:T(8,128)(2,1)S(1)}, bf16[128,8192]{1,0:T(8,128)(2,1)S(1)}, bf16[256,8192]{1,0:T(8,128)(2,1)S(1)}, f32[128,256]{1,0:T(8,128)S(1)}) custom-call(bf16[128,8192]{1,0:T(8,128)(2,1)} %movie_h.1, f32[16,128]{1,0:T(8,128)} %bitcast.6, bf16[8192,256]{1,0:T(8,128)(2,1)} %proj_h.1, bf16[256,8192]{1,0:T(8,128)(2,1)} %foot_h.1, ...), custom_call_target="tpu_custom_call" | custom-call | tf_op jit(solution)/shard_map/pallas_call | solution.py:458
  25.1 1.7 %shard_map.87 = (f32[32,128]{1,0:T(8,128)}, bf16[128,8192]{1,0:T(8,128)(2,1)}) custom-call(bf16[128,256]{1,0:T(8,128)(2,1)S(1)} %get-tuple-element.6.low_v, bf16[128,8192]{1,0:T(8,128)(2,1)S(1)} %get-tuple-element.7.warp_v, bf16[256,8192]{1,0:T(8,128)(2,1)S(1)} %get-tuple-element.8.foot_v, f32[128,256]{1,0:T(8,128)S(1)} %get-tuple-element.9.act_v), custom_call_target="tpu_custom_call" | custom-call | tf_op jit(solution)/shard_map/pallas_call | solution.py:509

commit v7 on v5

--- a/solution.py
+++ b/solution.py
@@ -44,7 +44,7 @@
     movie_v, proj_v, halo_v, shift_v, shifts_r, quality_r, cont_r, ret_r,
     col_v, rows_v, prefix_v, suffix_v, scale_v, coef_v, part_v,
     rs_v, all_v, tm_v, carry_v, out_v,
-    load_sem, halo_send, halo_recv, sems, ends_v, sent_v, enter_v, table_v, round_sem,
+    load_sem, halo_send, halo_recv, sems, ends_v, sent_v, enter_v, table_v, step_v, round_sem,
 ):
     frames, pixels = movie_v.shape
     factors = proj_v.shape[1]
@@ -362,20 +362,28 @@
     for j in (1, 0):
         for peer in peers + [me_s] * j:
             cs_copy(j, peer).start()
+    for h in halves:
+        for level in range(steps):
+            step_v[level, :, h] = col_v[level] * powers[level][:, h]
+            step_v[steps + level, :, h] = col_v[steps + level] * powers[level][:, h]
+
     def smoothed(x, h):
         fore = x
         back = x * (col_v[CONT] * ret[:, h])
         for level in range(steps):
             d = 1 << level
-            fore = fore + (col_v[level] * powers[level][:, h]) * row_turn(fore, d)
-            back = back + (col_v[steps + level] * powers[level][:, h]) * row_turn(back, -d)
+            fore = fore + step_v[level, :, h] * row_turn(fore, d)
+            back = back + step_v[steps + level, :, h] * row_turn(back, -d)
         row = lax.broadcasted_iota(jnp.int32, back.shape, 0)
         return fore + jnp.where(row < frames - 1, row_turn(back, -1), 0.0)
 
     for h in halves:
         norm = smoothed(col_v[QUALITY], h)
         norm = norm + prefix_v[:, h] * norm_in[:, h] + suffix_v[:, h] * norm_out[:, h]
-        scale_v[:, h] = 1.0 / jnp.sqrt(norm)
+        scale = 1.0 / jnp.sqrt(norm)
+        scale_v[:, h] = scale
+        prefix_v[:, h] *= scale
+        suffix_v[:, h] *= scale
 
     @pl.when(me_s < strip_n - 1)
     def _():
@@ -392,7 +400,7 @@
     settled(all_v, (strip_n - 1) * share, 5)
     sums = []
     for h in halves:
-        sums.append(smoothed(all_v[:, h].astype(F32) * col_v[QUALITY], h))
+        sums.append(smoothed(all_v[:, h].astype(F32) * col_v[QUALITY], h) * scale_v[:, h])
     settled(carry_v, len(planes) * strip_n - 1, 7)
     carried = carry_v[0]
     for i in range(1, len(planes) * strip_n):
@@ -400,7 +408,6 @@
     for i, h in enumerate(halves):
         j = len(halves) + i
         value = sums[i] + prefix_v[:, h] * carried[i : i + 1] + suffix_v[:, h] * carried[j : j + 1]
-        value = value * scale_v[:, h]
         out_v[h, :] = value.T
         low_v[:, h] = value.astype(BF16)
     per = factors // strip_n
@@ -477,6 +484,7 @@
             pltpu.VMEM((frames, factors), BF16),
             pltpu.VMEM((2, 2 * halves, 128), F32),
             pltpu.VMEM((2 * halves, tm_n, 128), F32),
+            pltpu.VMEM((2 * steps, frames, factors), F32),
             pltpu.SemaphoreType.REGULAR((ROUNDS,)),
         ],
         compiler_params=pltpu.CompilerParams(

time: 26.9 us -> 26.9 us (level)
  no operation moved by 1% of the time
where the time goes in v7:
time: 26.9 us; the launch traced here: 26.8 us
  Pallas kernels  26.2 us (97%)
  between operations  0.64 us (2%)
    pallas_call x1, Pallas kernels, body(): pl.pallas_call(functools.partial(kernel, tm_n, strip_n), out_shape=(pltpu...  24.5 us
    pallas_call x1, Pallas kernels, body(): pl.pallas_call(rebuild, out_shape=(jax.ShapeDtypeStruct((per, frames), F3...  1.66 us

profile of v7, /device:TPU:1, one launch (start us, length us, event | category | flops | bytes accessed | tf_op | source)
XLA Modules:
  0.0 26.8 jit_solution(5473417093727887433)
XLA Ops:
  0.6 24.5 %shard_map.86 = (bf16[128,256]{1,0:T(8,128)(2,1)S(1)}, bf16[128,8192]{1,0:T(8,128)(2,1)S(1)}, bf16[256,8192]{1,0:T(8,128)(2,1)S(1)}, f32[32,128]{1,0:T(8,128)S(1)}) custom-call(bf16[128,8192]{1,0:T(8,128)(2,1)} %movie_h.1, f32[16,128]{1,0:T(8,128)} %bitcast.6, bf16[8192,256]{1,0:T(8,128)(2,1)} %proj_h.1, bf16[256,8192]{1,0:T(8,128)(2,1)} %foot_h.1, ...), custom_call_target="tpu_custom_call" | custom-call | tf_op jit(solution)/shard_map/pallas_call | solution.py:450
  25.1 1.7 %shard_map.87 = (f32[32,128]{1,0:T(8,128)}, bf16[128,8192]{1,0:T(8,128)(2,1)}) custom-call(bf16[128,256]{1,0:T(8,128)(2,1)S(1)} %get-tuple-element.6.low_v, bf16[128,8192]{1,0:T(8,128)(2,1)S(1)} %get-tuple-element.7.warp_v, bf16[256,8192]{1,0:T(8,128)(2,1)S(1)} %get-tuple-element.8.foot_v, f32[32,128]{1,0:T(8,128)S(1)} %get-tuple-element.9.act_v), custom_call_target="tpu_custom_call" | custom-call | tf_op jit(solution)/shard_map/pallas_call | solution.py:503

commit v8 on v5

--- a/solution.py
+++ b/solution.py
@@ -160,7 +160,6 @@
         prefix = prefix * lane_shift(prefix, d, 1.0)
         suffix = suffix * lane_shift(suffix, -d, 1.0)
     after = lane_shift(suffix, -1, 1.0)
-    next_round(1)
     rows_v[0] = quality
     rows_v[1] = cont
     rows_v[2] = prefix
@@ -215,7 +214,7 @@
         at = slice(first * cols, last * cols)
         return jnp.dot(warp_v[:, at], proj_v[at, :], preferred_element_type=F32)
 
-    next_round(2)
+    next_round(1)
     for copy in large:
         copy.wait()
     group = 4
@@ -225,8 +224,7 @@
             warp_into(h, row_ref(h - 1), row_ref(h + 1))
         inner = project(first, last)
         part_v[...] = inner if first == 1 else part_v[...] + inner
-        if first == 1 + 2 * group:
-            next_round(3)
+    next_round(2)
     foot_load.start()
 
     swap = me_s // Y - me_s // (Y + 1)
@@ -297,6 +295,7 @@
         ends_v[i : i + 1] = jnp.sum(weighted * suffix_v[:, h], axis=0, keepdims=True)
         ends_v[j : j + 1] = jnp.sum(weighted * prefix_v[:, h], axis=0, keepdims=True)
     tm_v[place] = ends_v[...]
+    next_round(3)
     for dz in (4, 3, 5, 2, 6, 1, 7, 0):
         for dc in (1, 0):
             if dz or dc:

time: 26.9 us -> 26.8 us (level)
  no operation moved by 1% of the time
where the time goes in v8:
time: 26.8 us
  Pallas kernels  26.1 us (97%)
  between operations  0.64 us (2%)
    pallas_call x1, Pallas kernels, body(): pl.pallas_call(functools.partial(kernel, tm_n, strip_n), out_shape=(pltpu...  24.5 us
    pallas_call x1, Pallas kernels, body(): pl.pallas_call(rebuild, out_shape=(jax.ShapeDtypeStruct((per, frames), F3...  1.66 us

profile of v8, /device:TPU:1, one launch (start us, length us, event | category | flops | bytes accessed | tf_op | source)
XLA Modules:
  0.0 26.8 jit_solution(15074320320349339373)
XLA Ops:
  0.6 24.5 %shard_map.86 = (bf16[128,256]{1,0:T(8,128)(2,1)S(1)}, bf16[128,8192]{1,0:T(8,128)(2,1)S(1)}, bf16[256,8192]{1,0:T(8,128)(2,1)S(1)}, f32[32,128]{1,0:T(8,128)S(1)}) custom-call(bf16[128,8192]{1,0:T(8,128)(2,1)} %movie_h.1, f32[16,128]{1,0:T(8,128)} %bitcast.6, bf16[8192,256]{1,0:T(8,128)(2,1)} %proj_h.1, bf16[256,8192]{1,0:T(8,128)(2,1)} %foot_h.1, ...), custom_call_target="tpu_custom_call" | custom-call | tf_op jit(solution)/shard_map/pallas_call | solution.py:442
  25.1 1.7 %shard_map.87 = (f32[32,128]{1,0:T(8,128)}, bf16[128,8192]{1,0:T(8,128)(2,1)}) custom-call(bf16[128,256]{1,0:T(8,128)(2,1)S(1)} %get-tuple-element.6.low_v, bf16[128,8192]{1,0:T(8,128)(2,1)S(1)} %get-tuple-element.7.warp_v, bf16[256,8192]{1,0:T(8,128)(2,1)S(1)} %get-tuple-element.8.foot_v, f32[32,128]{1,0:T(8,128)S(1)} %get-tuple-element.9.act_v), custom_call_target="tpu_custom_call" | custom-call | tf_op jit(solution)/shard_map/pallas_call | solution.py:494
